TPU v7x, 512 devices: a whole 4x4x16 slice. The times are simulated.
512 devices in a mesh: row: 32 (over z, core), col: 16 (over y, x).
Axes of the slice: x: 4, y: 4, z: 16, core: 2. Of those that a mesh axis runs over, the one named last changes fastest.
Arguments:
- tokens: bfloat16 [512, 16384], P('col', 'row'), may hold values from -6 to 6
- query_weight: bfloat16 [16384, 8192], P('row', 'col'), may hold values from -0.09375 to 0.09375
- keyval_weight: bfloat16 [16384, 2048], P('row', 'col'), may hold values from -0.09375 to 0.09375
Outputs:
- query_proj: bfloat16 [512, 8192], P('row', 'col')
- query_code: bfloat16 [16384, 8192], P('row', 'col')
- query_scale: float32 [128, 64], P('row', 'col')
- keyval_code: bfloat16 [16384, 2048], P('row', 'col')
- keyval_scale: float32 [128, 16], P('row', 'col')
All inputs are finite; a program needn't handle non-finite values. Where the computation divides by a largest or mean magnitude, that divisor is 1e-20 or more.
Results may differ from a plain program's by a relative error of at most 0.0095.
Values may be sent and summed in bfloat16 or wider, within the bound.
No kernel may reach another device: no remote copies, remote signals or barrier semaphores. Data moves between devices by JAX's collectives and lax.ppermute only.
A program may use at most 64 MiB of HBM per device.

v0:
```python
import math

import jax
import jax.numpy as jnp
from jax import lax
from jax.sharding import PartitionSpec as P

BLOCK = 128
QSTEPS = 4


EPSILON = 1e-06
SOFTNESS = 0.9
TWO_PI = 2.0 * math.pi


def soften(argument):
    return argument - SOFTNESS * jnp.sin(TWO_PI * argument) / TWO_PI


def block_codes(weight, smooth):
    smoothed = weight.astype(jnp.float32) * smooth[:, None]
    height, breadth = smoothed.shape
    tile_view = smoothed.reshape(height // BLOCK, BLOCK, breadth // BLOCK, BLOCK)
    scales = (jnp.max(jnp.abs(tile_view), axis=(1, 3)) + EPSILON) / QSTEPS
    encoded = (
        soften(tile_view / scales[:, None, :, None]).reshape(height, breadth).astype(jnp.bfloat16)
    )
    return (encoded, scales)


def token_encode(x_smooth, row_peak):
    token_scale = ((row_peak + EPSILON) / QSTEPS).astype(jnp.bfloat16)
    encoded = soften(x_smooth / token_scale.astype(jnp.float32)[:, None]).astype(jnp.bfloat16)
    return (encoded, token_scale)


def body(tokens, query_weight, keyval_weight):
    act_local = jnp.max(jnp.abs(tokens), axis=0).astype(jnp.float32)
    weight_local = jnp.maximum(
        jnp.max(jnp.abs(query_weight), axis=1), jnp.max(jnp.abs(keyval_weight), axis=1)
    ).astype(jnp.float32)
    act_peak, weight_peak = lax.pmax((act_local, weight_local), "col")
    smooth = jnp.sqrt((act_peak + EPSILON) / (weight_peak + EPSILON))
    query_code, query_scale = block_codes(query_weight, smooth)
    keyval_code, keyval_scale = block_codes(keyval_weight, smooth)
    x_smooth = tokens.astype(jnp.float32) / smooth[None, :]
    row_peak = lax.pmax(jnp.max(jnp.abs(x_smooth), axis=1), "row")
    local_code, local_scale = token_encode(x_smooth, row_peak)
    x_code, token_scale = (
        lax.all_gather(local_code, "col", axis=0, tiled=True),
        lax.all_gather(local_scale, "col", axis=0, tiled=True),
    )
    column_scale = jnp.repeat(query_scale, BLOCK, axis=1)
    block_total = query_code.shape[0] // BLOCK
    out_width = query_code.shape[1]
    own_rows = x_code.shape[0] // lax.axis_size("row")
    scale_rows = token_scale.astype(jnp.float32)

    def add_block(block_index, running):
        code_block = lax.dynamic_slice_in_dim(x_code, block_index * BLOCK, BLOCK, 1)
        weight_block = lax.dynamic_slice_in_dim(query_code, block_index * BLOCK, BLOCK, 0)
        scale_row = lax.dynamic_slice_in_dim(column_scale, block_index, 1, 0)
        product = jnp.dot(code_block, weight_block, preferred_element_type=jnp.float32)
        return running + product * scale_row

    running = lax.fori_loop(
        0,
        block_total,
        add_block,
        jnp.zeros((own_rows * lax.axis_size("row"), out_width), jnp.float32),
    )
    query_proj = lax.psum_scatter(
        running * scale_rows[:, None], "row", scatter_dimension=0, tiled=True
    ).astype(jnp.bfloat16)
    return (query_proj, query_code, query_scale, keyval_code, keyval_scale)


def solution(mesh):
    in_specs = (P("col", "row"), P("row", "col"), P("row", "col"))
    out_specs = (
        P("row", "col"),
        P("row", "col"),
        P("row", "col"),
        P("row", "col"),
        P("row", "col"),
    )
    return jax.shard_map(body, mesh=mesh, in_specs=in_specs, out_specs=out_specs, check_vma=False)
```

profile of v0, /device:TPU:2, one launch (start us, length us, event | category | flops | bytes accessed | tf_op | source)
XLA Modules:
  0.0 286.5 jit_solution(13215520289935664740)
XLA Ops:
  7.2 0.0 copy-start
  7.2 0.0 reduce-scatter.2.cloned.1.call-start
  7.2 1.3 abs_reduce_fusion
  8.5 0.0 copy-start.3
  8.5 1.0 abs_reduce_fusion.2
  9.5 0.0 copy-done.3
  9.6 41.3 %all-reduce.1 = (f32[512]{0:T(512)S(1)}, f32[512]{0:T(512)S(1)}) all-reduce(f32[512]{0:T(512)S(1)} %maximum_convert_fusion, bf16[512]{0:T(512)(128)(2,1)S(1)} %abs_reduce_fusion.3), channel_id=1, replica_groups=mesh['row'=32,'col'=16] {'col'}, use_global_device_ids=true, to_apply=%region_4.0 | all-reduce | flops 1024 | bytes 7168 | tf_op jit(solution)/shard_map/pmax | solution.py:43
  50.9 0.0 copy-done
  50.9 0.2 fusion.4
  51.1 0.1 fusion.6
  51.2 1.3 abs.29
  52.6 1.5 reduce_max.65
  54.1 0.0 copy-start.4
  54.1 0.1 broadcast_bitcast_fusion
  54.2 0.5 copy-done.4
  54.7 0.2 div.84
  54.9 4.0 %subtract_convert_fusion = bf16[512,512]{1,0:T(8,128)(2,1)S(1)} fusion(f32[64,8,4,128]{3,2,1,0:T(4,128)S(1)} %bitcast.21, bf16[512,512]{1,0:T(8,128)(2,1)S(1)} %copy-done, f32[512]{0:T(512)S(1)} %fusion.7), kind=kLoop, calls=%fused_computation.7 | loop fusion | flops 1835008 | bytes 2099200 | tf_op jit(solution)/shard_map/convert_element_type | solution.py:27
  58.9 47.3 %pmax.23 = f32[32]{0:T(128)S(1)} all-reduce(f32[32]{0:T(128)S(1)} %fusion.6), channel_id=1, replica_groups=mesh['row'=32,'col'=16] {'row'}, use_global_device_ids=true, to_apply=%region_6.0 | all-reduce | flops 32 | bytes 256 | tf_op jit(solution)/shard_map/pmax | solution.py:48
  106.2 0.3 subtract_convert_fusion.2
  106.6 25.4 %all_gather.6 = bf16[512,512]{1,0:T(8,128)(2,1)S(1)} all-gather(bf16[32,512]{1,0:T(8,128)(2,1)S(1)} %subtract_convert_fusion.2), channel_id=1, replica_groups=mesh['row'=32,'col'=16] {'col'}, dimensions={0}, use_global_device_ids=true | all-gather | bytes 557056 | tf_op jit(solution)/shard_map/all_gather | solution.py:51
  132.0 1.9 while.14
  132.0 0.4 fusion.15
  132.5 0.4 fusion.15
  133.0 0.4 fusion.15
  133.5 0.4 fusion.15
  133.9 0.0 copy-start.1
  133.9 1.3 dynamic-slice
  135.9 0.2 dynamic-update-slice
  136.1 35.7 %all-reduce = bf16[512]{0:T(512)(128)(2,1)S(1)} all-reduce(bf16[512]{0:T(512)(128)(2,1)S(1)} %dynamic-update-slice), channel_id=1, replica_groups=mesh['row'=32,'col'=16] {'col'}, use_global_device_ids=true, to_apply=%add | all-reduce | flops 512 | bytes 2048
  171.9 1.1 broadcast_multiply_fusion
  173.0 0.0 copy-done.1
  173.0 0.0 copy-start.2
  173.0 0.0 reduce-scatter.2.cloned.1.call-update
  173.0 0.9 copy-done.2
  173.9 0.2 abs_reduce_fusion.1
  174.1 0.1 bitcast_reduce_fusion
  174.2 0.5 fusion.9
  174.8 0.1 broadcast_bitcast_fusion.1
  174.8 1.7 subtract_convert_fusion.1
  176.5 101.8 %reduce-scatter.2.cloned.1.call-done = f32[16,512]{1,0:T(8,128)} async-done(((f32[512,512]{1,0:T(8,128)}), f32[16,512]{1,0:T(8,128)}) %reduce-scatter.2.cloned.1.call-update) | async-done | bytes 32784 | tf_op jit(solution)/shard_map/reduce_scatter | solution.py:73
  278.3 1.4 convert_element_type.45
  (13 shorter events, 0.1 us)
Async XLA Ops:
  7.2 43.8 %copy-start = (bf16[512,512]{1,0:T(8,128)(2,1)S(1)}, bf16[512,512]{1,0:T(8,128)(2,1)}, u32[]{:S(2)}) copy-start(bf16[512,512]{1,0:T(8,128)(2,1)} %param.6) | copy-start | bytes 1572868
  7.2 271.1 %reduce-scatter.2.cloned.1.call-start = ((), (), s32[]{:S(2)}) async-start(), calls=%async_computation.1 | async-start | bytes 1081344 | tf_op jit(solution)/shard_map/reduce_scatter | solution.py:73
  8.5 1.0 copy-start.3
  54.1 0.6 copy-start.4
  133.9 39.1 %copy-start.1 = (bf16[512,512]{1,0:T(8,128)(2,1)}, bf16[512,512]{1,0:T(8,128)(2,1)S(1)}, u32[]{:S(2)}) copy-start(bf16[512,512]{1,0:T(8,128)(2,1)S(1)} %get-tuple-element.195) | copy-start | bytes 1572868
  173.0 0.9 copy-start.2
Sparse Core Ops, SparseCore 0:
  173.1 105.1 reduce-scatter.1
where the time goes:
time: 287 us
  blocking collectives  150 us (52%)
  waiting for transfers between devices  102 us (36%)
  between operations  14.8 us (5%)
  other arithmetic  13.5 us (5%)
  local copies, waits for them, and re-layouts  4.68 us (2%)
    reduce_scatter x1, waiting for transfers between devices, body(): lax.psum_scatter(running * scale_rows[:, None], 'row', scatter_dimension=...  102 us
    pmax x1, blocking collectives, body(): row_peak = lax.pmax(jnp.max(jnp.abs(x_smooth), axis=1), 'row')  47.3 us
    pmax x1, blocking collectives, body(): act_peak, weight_peak = lax.pmax((act_local, weight_local), 'col')  41.3 us
    unnamed x1, blocking collectives  35.7 us
    all_gather x1, blocking collectives, body(): lax.all_gather(local_code, 'col', axis=0, tiled=True)  25.4 us
  transfers between devices with their start and end apart: 1, of which 1 were waited for; matrix products, arithmetic and copies ran while one was open for 1% of the time, Pallas kernels for 0%

commit v1 on v0

v1 whole, which is shorter than its diff:
```python
import functools

import jax
import jax.numpy as jnp
from jax import lax
from jax.experimental import pallas as pl
from jax.experimental.pallas import tpu as pltpu
from jax.sharding import Mesh, PartitionSpec as P

BLOCK = 128
QSTEPS = 4
EPSILON = 1e-06
ROUNDER = 12582912.0
SINE = (
    0.8999999761581421,
    -5.921761989593506,
    11.689058303833008,
    -10.986687660217285,
    6.018372535705566,
    -2.1297717094421387,
    0.45832234621047974,
)
VMEM = pl.BlockSpec(memory_space=pltpu.VMEM)


def soften(value):
    offset = value - ((value + ROUNDER) - ROUNDER)
    square = offset * offset
    series = SINE[-1]
    for term in SINE[-2::-1]:
        series = series * square + term
    return value - offset * series


def across(column_major):
    return jnp.max(column_major.T, axis=0, keepdims=True)


def down(row):
    return jnp.broadcast_to(row, (BLOCK, BLOCK)).T


def peaks_kernel(tokens_ref, query_ref, keyval_ref, out_ref):
    depth = query_ref.shape[0]
    tokens = tokens_ref[...]
    rows = tokens.shape[0]
    peaks = []
    for base in range(0, depth, BLOCK):
        top = jnp.abs(keyval_ref[base : base + BLOCK, :])
        for left in range(0, query_ref.shape[1], BLOCK):
            top = jnp.maximum(top, jnp.abs(query_ref[base : base + BLOCK, left : left + BLOCK]))
        peaks.append(across(top.astype(jnp.float32)))
    peak = jnp.broadcast_to(jnp.concatenate(peaks, axis=1), (8, depth)).astype(jnp.bfloat16)
    for copy in range(out_ref.shape[0]):
        out_ref[copy, :rows, :] = tokens
        out_ref[copy, rows:, :] = peak


def smooth_kernel(gathered_ref, smooth_ref, out_ref):
    members, padded, depth = gathered_ref.shape
    rows = padded - 8
    act = jnp.abs(gathered_ref[0, :rows, :])
    weight = gathered_ref[0, rows:, :]
    for member in range(1, members):
        act = jnp.maximum(act, jnp.abs(gathered_ref[member, :rows, :]))
        weight = jnp.maximum(weight, gathered_ref[member, rows:, :])
    act_peak = jnp.max(act.astype(jnp.float32), axis=0, keepdims=True)
    weight_peak = jnp.max(weight.astype(jnp.float32), axis=0, keepdims=True)
    smooth = jnp.sqrt((act_peak + EPSILON) / (weight_peak + EPSILON))
    inverse = 1.0 / smooth
    smooth_ref[0:1, :] = smooth
    smooth_ref[1:2, :] = inverse
    per_block = BLOCK // rows
    lines = []
    for first in range(0, members, per_block):
        top = None
        for left in range(0, depth, BLOCK):
            piece = jnp.abs(gathered_ref[first : first + per_block, :rows, left : left + BLOCK])
            piece = piece.astype(jnp.float32).reshape(BLOCK, BLOCK) * inverse[:, left : left + BLOCK]
            top = piece if top is None else jnp.maximum(top, piece)
        lines.append(across(top))
    peak = jnp.concatenate(lines, axis=0)
    for copy in range(out_ref.shape[0]):
        out_ref[copy] = peak


def weights_kernel(query_ref, keyval_ref, smooth_ref, query_out, query_scale, keyval_out, keyval_scale):
    smooth = smooth_ref[0:1, :]
    for source, code_ref, scale_ref in (
        (query_ref, query_out, query_scale),
        (keyval_ref, keyval_out, keyval_scale),
    ):
        for row, base in enumerate(range(0, source.shape[0], BLOCK)):
            factor = down(smooth[:, base : base + BLOCK])
            for column, left in enumerate(range(0, source.shape[1], BLOCK)):
                block = source[base : base + BLOCK, left : left + BLOCK].astype(jnp.float32) * factor
                top = jnp.max(jnp.max(jnp.abs(block), axis=0, keepdims=True), axis=1, keepdims=True)
                scale = (top + EPSILON) / QSTEPS
                scale_ref[row : row + 1, column : column + 1] = scale
                code = soften(block * (1.0 / scale)).astype(jnp.bfloat16)
                code_ref[base : base + BLOCK, left : left + BLOCK] = code


def project_kernel(core_ref, gathered_ref, smooth_ref, peaks_ref, code_ref, scale_ref, send_ref, keep_ref):
    members, padded, depth = gathered_ref.shape
    rows = padded - 8
    half = rows // 2
    peak = peaks_ref[0]
    for member in range(1, peaks_ref.shape[0]):
        peak = jnp.maximum(peak, peaks_ref[member])
    scale = ((peak + EPSILON) / QSTEPS).astype(jnp.bfloat16).astype(jnp.float32)
    inverse = smooth_ref[1:2, :]
    per_block = BLOCK // rows
    core = core_ref[0]
    blocks = depth // BLOCK
    column_scale = []
    for a in range(blocks):
        column_scale.append(
            jnp.concatenate(
                [
                    jnp.broadcast_to(scale_ref[a : a + 1, c : c + 1], (1, BLOCK))
                    for c in range(scale_ref.shape[1])
                ],
                axis=1,
            )
        )
    for index, first in enumerate(range(0, members, per_block)):
        row_scale = down(scale[index : index + 1, :])
        row_inverse = 1.0 / row_scale
        total = None
        for a in range(blocks):
            left = a * BLOCK
            piece = gathered_ref[first : first + per_block, :rows, left : left + BLOCK]
            piece = piece.astype(jnp.float32).reshape(BLOCK, BLOCK)
            value = piece * inverse[:, left : left + BLOCK] * row_inverse
            code = soften(value).astype(jnp.bfloat16)
            product = jnp.dot(
                code, code_ref[left : left + BLOCK, :], preferred_element_type=jnp.float32
            )
            product = product * column_scale[a]
            total = product if total is None else total + product
        width = total.shape[1]
        total = jnp.concatenate(
            [total[:, c : c + BLOCK] * row_scale for c in range(0, width, BLOCK)], axis=1
        )
        total = total.reshape(per_block, 2, half, width)
        low, high = total[:, 0], total[:, 1]
        first_core = core == 0
        send_ref[first : first + per_block] = jnp.where(first_core, high, low)
        keep_ref[first : first + per_block] = jnp.where(first_core, low, high)


def join_kernel(keep_ref, other_ref, out_ref):
    out_ref[...] = (keep_ref[...] + other_ref[...]).astype(out_ref.dtype)


def sum_kernel(parts_ref, out_ref):
    total = parts_ref[0].astype(jnp.float32)
    for part in range(1, parts_ref.shape[0]):
        total = total + parts_ref[part].astype(jnp.float32)
    out_ref[...] = total.astype(out_ref.dtype)


def call(kernel, out_shape, args, flops=0, specs=None, name=None):
    outs = out_shape if isinstance(out_shape, (tuple, list)) else (out_shape,)
    moved = sum(a.size * a.dtype.itemsize for a in (*args, *outs))
    return pl.pallas_call(
        kernel,
        out_shape=out_shape,
        in_specs=specs or [VMEM] * len(args),
        out_specs=jax.tree.map(lambda _: VMEM, out_shape),
        cost_estimate=pl.CostEstimate(flops=flops, bytes_accessed=moved, transcendentals=0),
        name=name,
    )(*args)


def exchange(array, axes):
    return lax.all_to_all(array, axes, 0, 0, tiled=True)


def body(chips, columns, tokens, query_weight, keyval_weight):
    f32, bf16 = jnp.float32, jnp.bfloat16
    shape = jax.ShapeDtypeStruct
    rows, depth = tokens.shape
    width = query_weight.shape[1]
    send = call(
        peaks_kernel, shape((columns, rows + 8, depth), bf16), (tokens, query_weight, keyval_weight),
        name="peaks",
    )
    gathered = exchange(send, ("y", "x"))
    smooth, row_peaks = call(
        smooth_kernel,
        (shape((8, depth), f32), shape((2 * chips, depth // BLOCK, BLOCK), f32)),
        (gathered,),
        name="smooth",
    )
    peaks = exchange(row_peaks, ("z", "core"))
    query_code, query_scale, keyval_code, keyval_scale = call(
        weights_kernel,
        (
            shape(query_weight.shape, bf16),
            shape((depth // BLOCK, width // BLOCK), f32),
            shape(keyval_weight.shape, bf16),
            shape((depth // BLOCK, keyval_weight.shape[1] // BLOCK), f32),
        ),
        (query_weight, keyval_weight, smooth),
        flops=20 * (query_weight.size + keyval_weight.size),
        name="weights",
    )
    half = shape((columns, rows // 2, width), f32)
    core = lax.axis_index("core").astype(jnp.int32).reshape(1)
    to_other, kept = call(
        project_kernel,
        (half, half),
        (core, gathered, smooth, peaks, query_code, query_scale),
        specs=[pl.BlockSpec(memory_space=pltpu.SMEM)] + [VMEM] * 5,
        flops=2 * columns * rows * depth * width,
        name="project",
    )
    from_other = lax.ppermute(to_other, "core", [(0, 1), (1, 0)])
    joined = call(join_kernel, shape(half.shape, bf16), (kept, from_other), name="join")
    parts = exchange(joined, "z")
    query_proj = call(sum_kernel, shape((rows // 2, width), bf16), (parts,), name="sum")
    return (query_proj, query_code, query_scale, keyval_code, keyval_scale)


def solution(mesh):
    rows, columns = mesh.devices.shape
    chips = rows // 2
    side = int(round(columns**0.5))
    fine = Mesh(
        mesh.devices.reshape(chips, 2, columns // side, side), ("z", "core", "y", "x")
    )
    row, col = ("z", "core"), ("y", "x")
    return jax.shard_map(
        functools.partial(body, chips, columns),
        mesh=fine,
        in_specs=(P(col, row), P(row, col), P(row, col)),
        out_specs=(P(row, col),) * 5,
        check_vma=False,
    )
```

time: 287 us -> 90.9 us (0.32)
  the two profiles are of different devices: /device:TPU:2 before, /device:TPU:32 now
where the time goes in v1:
time: 90.9 us; the launch traced here: 90.3 us
  waiting for transfers between devices  30.5 us (34%)
  starting transfers between devices  22.2 us (24%)
  blocking collectives  20.1 us (22%)
  Pallas kernels  14.2 us (16%)
  local copies, waits for them, and re-layouts  2.71 us (3%)
    all_to_all x2, waiting for transfers between devices, exchange(): return lax.all_to_all(array, axes, 0, 0, tiled=True)  28.4 us
    all_to_all x2, starting transfers between devices, exchange(): return lax.all_to_all(array, axes, 0, 0, tiled=True)  20.3 us
    all_to_all x1, blocking collectives, exchange(): return lax.all_to_all(array, axes, 0, 0, tiled=True)  20.1 us
    pallas_call x6, Pallas kernels, call(): pl.pallas_call(kernel, out_shape=out_shape, in_specs=specs or [VMEM] * le...  14.2 us
    unnamed x9, local copies, waits for them, and re-layouts  2.71 us
    ppermute x1, waiting for transfers between devices, body(): from_other = lax.ppermute(to_other, 'core', [(0, 1), (1, 0)])  2.09 us
    ppermute x1, starting transfers between devices, body(): from_other = lax.ppermute(to_other, 'core', [(0, 1), (1, 0)])  1.91 us
  transfers between devices with their start and end apart: 3, of which 3 were waited for; matrix products, arithmetic and copies ran while one was open for 1% of the time, Pallas kernels for 3%

profile of v1, /device:TPU:32, one launch (start us, length us, event | category | flops | bytes accessed | tf_op | source)
XLA Modules:
  0.0 90.3 jit_solution(9988523721661391241)
XLA Ops:
  0.6 2.1 %peaks.1 = bf16[16,40,512]{2,1,0:T(8,128)(2,1)} custom-call(bf16[32,512]{1,0:T(8,128)(2,1)} %tokens_ref.1, bf16[512,512]{1,0:T(8,128)(2,1)} %query_ref.3, bf16[512,128]{1,0:T(8,128)(2,1)} %keyval_ref.3), custom_call_target="tpu_custom_call" | custom-call | bytes 1343488 | tf_op jit(solution)/shard_map/peaks/pallas_call | solution.py:167
  2.8 20.1 %all_to_all.15.gathered_ref = bf16[16,40,512]{2,1,0:T(8,128)(2,1)} all-to-all(bf16[16,40,512]{2,1,0:T(8,128)(2,1)} %peaks.1), channel_id=1, replica_groups=mesh['z'=16,'core'=2,'y'=4,'x'=4] {'y','x'}, dimensions={0} | all-to-all | bytes 1310720 | tf_op jit(solution)/shard_map/all_to_all | solution.py:178
  22.8 2.0 %smooth.1 = (f32[8,512]{1,0:T(8,128)}, f32[32,4,128]{2,1,0:T(4,128)}) custom-call(bf16[16,40,512]{2,1,0:T(8,128)(2,1)} %all_to_all.15.gathered_ref), custom_call_target="tpu_custom_call" | custom-call | bytes 737280 | tf_op jit(solution)/shard_map/smooth/pallas_call | solution.py:167
  24.8 15.4 %all-to-all-start.1 = ((f32[32,4,128]{2,1,0:T(4,128)}), f32[32,4,128]{2,1,0:T(4,128)S(1)}, u32[]{:S(2)}, u32[]{:S(2)}) async-start(f32[32,4,128]{2,1,0:T(4,128)} %get-tuple-element.14), calls=%async_computation.1 | async-start | bytes 131072 | tf_op jit(solution)/shard_map/all_to_all | solution.py:178
  40.2 2.9 %weights.1 = (bf16[512,512]{1,0:T(8,128)(2,1)}, f32[4,4]{1,0:T(4,128)}, bf16[512,128]{1,0:T(8,128)(2,1)}, f32[4,1]{1,0:T(4,128)}) custom-call(bf16[512,512]{1,0:T(8,128)(2,1)} %query_ref.3, bf16[512,128]{1,0:T(8,128)(2,1)} %keyval_ref.3, f32[8,512]{1,0:T(8,128)} %get-tuple-element.13.smooth_ref), custom_call_target="tpu_custom_call" | custom-call | flops 6553600 | bytes 1327184 | tf_op jit(solution)/shard_map/weights/pallas_call | solution.py:167
  43.1 10.2 %all-to-all-done.1.peaks_ref = f32[32,4,128]{2,1,0:T(4,128)S(1)} async-done(((f32[32,4,128]{2,1,0:T(4,128)}), f32[32,4,128]{2,1,0:T(4,128)S(1)}, u32[]{:S(2)}, u32[]{:S(2)}) %all-to-all-start.1) | async-done | bytes 65568 | tf_op jit(solution)/shard_map/all_to_all | solution.py:178
  53.3 0.0 copy-start.2
  53.3 0.6 copy-done.2
  53.9 3.6 %project.1 = (f32[16,16,512]{2,1,0:T(8,128)}, f32[16,16,512]{2,1,0:T(8,128)}) custom-call(s32[1]{0:T(128)} %bitcast.core_ref, bf16[16,40,512]{2,1,0:T(8,128)(2,1)} %all_to_all.15.gathered_ref, f32[8,512]{1,0:T(8,128)} %get-tuple-element.13.smooth_ref, f32[32,4,128]{2,1,0:T(4,128)} %copy-done.2, bf16[512,512]{1,0:T(8,128)(2,1)} %get-tuple-element.22.code_ref, ...), custom_call_target="tpu_custom_call" | custom-call | flops 268435456 | bytes 2310212 | tf_op jit(solution)/shard_map/project/pallas_call | solution.py:167
  57.5 1.9 %collective-permute-start = (f32[16,16,512]{2,1,0:T(8,128)}, f32[16,16,512]{2,1,0:T(8,128)S(1)}, u32[]{:S(2)}, u32[]{:S(2)}) collective-permute-start(f32[16,16,512]{2,1,0:T(8,128)} %get-tuple-element.18), channel_id=1, source_target_pairs={{0,16},{16,0},{1,17},{17,1},{2,18},{18,2},{3,19},{19,3},{4,20},{20... | collective-permute-start | bytes 1572872 | tf_op jit(solution)/shard_map/ppermute | solution.py:220
  59.4 2.1 %collective-permute-done.other_ref = f32[16,16,512]{2,1,0:T(8,128)S(1)} collective-permute-done((f32[16,16,512]{2,1,0:T(8,128)}, f32[16,16,512]{2,1,0:T(8,128)S(1)}, u32[]{:S(2)}, u32[]{:S(2)}) %collective-permute-start) | collective-permute-done | bytes 524320 | tf_op jit(solution)/shard_map/ppermute | solution.py:220
  61.5 0.0 copy-start.1
  61.5 0.8 copy-done.1
  62.3 2.0 %join.1 = bf16[16,16,512]{2,1,0:T(8,128)(2,1)} custom-call(f32[16,16,512]{2,1,0:T(8,128)} %get-tuple-element.17.keep_ref, f32[16,16,512]{2,1,0:T(8,128)} %copy-done.1), custom_call_target="tpu_custom_call" | custom-call | bytes 1310720 | tf_op jit(solution)/shard_map/join/pallas_call | solution.py:167
  64.3 0.0 copy-start.3
  64.3 4.9 %all-to-all-start.2 = ((bf16[16,16,512]{2,1,0:T(8,128)(2,1)}), bf16[16,16,512]{2,1,0:T(8,128)(2,1)S(1)}, u32[]{:S(2)}, u32[]{:S(2)}) async-start(bf16[16,16,512]{2,1,0:T(8,128)(2,1)} %join.1), calls=%async_computation.2 | async-start | bytes 524288 | tf_op jit(solution)/shard_map/all_to_all | solution.py:178
  69.2 0.0 copy-done.3
  69.2 0.6 copy.8
  69.8 18.2 %all-to-all-done.2.parts_ref = bf16[16,16,512]{2,1,0:T(8,128)(2,1)S(1)} async-done(((bf16[16,16,512]{2,1,0:T(8,128)(2,1)}), bf16[16,16,512]{2,1,0:T(8,128)(2,1)S(1)}, u32[]{:S(2)}, u32[]{:S(2)}) %all-to-all-start.2) | async-done | bytes 262176 | tf_op jit(solution)/shard_map/all_to_all | solution.py:178
  88.0 0.0 copy-start
  88.0 0.7 copy-done
  88.7 1.6 %sum.1 = bf16[16,512]{1,0:T(8,128)(2,1)} custom-call(bf16[16,16,512]{2,1,0:T(8,128)(2,1)} %copy-done), custom_call_target="tpu_custom_call" | custom-call | bytes 278528 | tf_op jit(solution)/shard_map/sum/pallas_call | solution.py:167
Async XLA Ops:
  24.8 28.5 %all-to-all-start.1 = ((f32[32,4,128]{2,1,0:T(4,128)}), f32[32,4,128]{2,1,0:T(4,128)S(1)}, u32[]{:S(2)}, u32[]{:S(2)}) async-start(f32[32,4,128]{2,1,0:T(4,128)} %get-tuple-element.14), calls=%async_computation.1 | async-start | bytes 131072 | tf_op jit(solution)/shard_map/all_to_all | solution.py:178
  53.3 0.6 copy-start.2
  57.5 4.0 %collective-permute-start = (f32[16,16,512]{2,1,0:T(8,128)}, f32[16,16,512]{2,1,0:T(8,128)S(1)}, u32[]{:S(2)}, u32[]{:S(2)}) collective-permute-start(f32[16,16,512]{2,1,0:T(8,128)} %get-tuple-element.18), channel_id=1, source_target_pairs={{0,16},{16,0},{1,17},{17,1},{2,18},{18,2},{3,19},{19,3},{4,20},{20... | collective-permute-start | bytes 1572872 | tf_op jit(solution)/shard_map/ppermute | solution.py:220
  61.5 0.8 copy-start.1
  64.3 4.9 %copy-start.3 = (f32[4,1]{1,0:T(4,128)S(1)}, f32[4,1]{1,0:T(4,128)}, u32[]{:S(2)}) copy-start(f32[4,1]{1,0:T(4,128)} %get-tuple-element.25) | copy-start | bytes 52
  64.3 23.7 %all-to-all-start.2 = ((bf16[16,16,512]{2,1,0:T(8,128)(2,1)}), bf16[16,16,512]{2,1,0:T(8,128)(2,1)S(1)}, u32[]{:S(2)}, u32[]{:S(2)}) async-start(bf16[16,16,512]{2,1,0:T(8,128)(2,1)} %join.1), calls=%async_computation.2 | async-start | bytes 524288 | tf_op jit(solution)/shard_map/all_to_all | solution.py:178
  88.0 0.7 copy-start

commit v2 on v1

--- a/solution.py
+++ b/solution.py
@@ -170,6 +170,7 @@
         in_specs=specs or [VMEM] * len(args),
         out_specs=jax.tree.map(lambda _: VMEM, out_shape),
         cost_estimate=pl.CostEstimate(flops=flops, bytes_accessed=moved, transcendentals=0),
+        compiler_params=pltpu.CompilerParams(vmem_limit_bytes=8 << 20),
         name=name,
     )(*args)
 

time: 90.9 us -> 85.2 us (0.937)
  Pallas kernels: 14.2 us -> 5.61 us
  local copies, waits for them, and re-layouts: 2.71 us -> 5.02 us
    pallas_call x6, Pallas kernels: 14.2 us -> 5.61 us  [call(): pl.pallas_call(kernel, out_shape=out_shape, in_specs=specs or [VMEM] * le...]
    unnamed x9 -> x15, local copies, waits for them, and re-layouts: 2.71 us -> 5.02 us
    all_to_all x2, waiting for transfers between devices: 28.4 us -> 29.6 us  [exchange(): return lax.all_to_all(array, axes, 0, 0, tiled=True)]
  transfers between devices with their start and end apart: 3 -> 3, of which waited for: 3 -> 3; matrix products, arithmetic and copies ran while one was open for 1% -> 1% of each run, Pallas kernels for 3% -> 2%
where the time goes in v2:
time: 85.2 us; the launch traced here: 84.7 us
  waiting for transfers between devices  31.4 us (37%)
  starting transfers between devices  22.2 us (26%)
  blocking collectives  19.8 us (23%)
  Pallas kernels  5.61 us (7%)
  local copies, waits for them, and re-layouts  5.02 us (6%)
    all_to_all x2, waiting for transfers between devices, exchange(): return lax.all_to_all(array, axes, 0, 0, tiled=True)  29.6 us
    all_to_all x2, starting transfers between devices, exchange(): return lax.all_to_all(array, axes, 0, 0, tiled=True)  20.3 us
    all_to_all x1, blocking collectives, exchange(): return lax.all_to_all(array, axes, 0, 0, tiled=True)  19.8 us
    pallas_call x6, Pallas kernels, call(): pl.pallas_call(kernel, out_shape=out_shape, in_specs=specs or [VMEM] * le...  5.61 us
    unnamed x15, local copies, waits for them, and re-layouts  5.02 us
    ppermute x1, starting transfers between devices, body(): from_other = lax.ppermute(to_other, 'core', [(0, 1), (1, 0)])  1.92 us
    ppermute x1, waiting for transfers between devices, body(): from_other = lax.ppermute(to_other, 'core', [(0, 1), (1, 0)])  1.88 us
  transfers between devices with their start and end apart: 3, of which 3 were waited for; matrix products, arithmetic and copies ran while one was open for 1% of the time, Pallas kernels for 2%

profile of v2, /device:TPU:32, one launch (start us, length us, event | category | flops | bytes accessed | tf_op | source)
XLA Modules:
  0.0 84.7 jit_solution(10301930845872334224)
XLA Ops:
  0.6 0.0 copy-start
  0.6 1.0 %copy-done = bf16[512,512]{1,0:T(8,128)(2,1)S(1)} copy-done((bf16[512,512]{1,0:T(8,128)(2,1)S(1)}, bf16[512,512]{1,0:T(8,128)(2,1)}, u32[]{:S(2)}) %copy-start) | copy-done | bytes 524312
  1.7 0.0 copy-start.3
  1.7 0.9 %copy-done.3 = bf16[512,128]{1,0:T(8,128)(2,1)S(1)} copy-done((bf16[512,128]{1,0:T(8,128)(2,1)S(1)}, bf16[512,128]{1,0:T(8,128)(2,1)}, u32[]{:S(2)}) %copy-start.3) | copy-done | bytes 131096
  2.6 0.0 copy-start.5
  2.6 0.8 copy-done.5
  3.3 0.2 peaks.1
  3.5 19.8 %all_to_all.15.gathered_ref = bf16[16,40,512]{2,1,0:T(8,128)(2,1)S(1)} all-to-all(bf16[16,40,512]{2,1,0:T(8,128)(2,1)S(1)} %peaks.1), channel_id=1, replica_groups=mesh['z'=16,'core'=2,'y'=4,'x'=4] {'y','x'}, dimensions={0} | all-to-all | bytes 1310720 | tf_op jit(solution)/shard_map/all_to_all | solution.py:179
  23.3 0.0 copy-start.1
  23.3 0.9 %smooth.1 = (f32[8,512]{1,0:T(8,128)S(1)}, f32[32,4,128]{2,1,0:T(4,128)}) custom-call(bf16[16,40,512]{2,1,0:T(8,128)(2,1)S(1)} %all_to_all.15.gathered_ref), custom_call_target="tpu_custom_call" | custom-call | bytes 737280 | tf_op jit(solution)/shard_map/smooth/pallas_call | solution.py:167
  24.2 0.0 copy-start.4
  24.2 15.5 %all-to-all-start.1 = ((f32[32,4,128]{2,1,0:T(4,128)}), f32[32,4,128]{2,1,0:T(4,128)S(1)}, u32[]{:S(2)}, u32[]{:S(2)}) async-start(f32[32,4,128]{2,1,0:T(4,128)} %get-tuple-element.14), calls=%async_computation.1 | async-start | bytes 131072 | tf_op jit(solution)/shard_map/all_to_all | solution.py:179
  39.7 0.0 copy-done.1
  39.7 0.0 copy-done.4
  39.7 1.8 %weights.1 = (bf16[512,512]{1,0:T(8,128)(2,1)}, f32[4,4]{1,0:T(4,128)}, bf16[512,128]{1,0:T(8,128)(2,1)}, f32[4,1]{1,0:T(4,128)S(1)}) custom-call(bf16[512,512]{1,0:T(8,128)(2,1)S(1)} %copy-done.1, bf16[512,128]{1,0:T(8,128)(2,1)S(1)} %copy-done.4, f32[8,512]{1,0:T(8,128)S(1)} %get-tuple-element.13.smooth_ref), custom_call_target="tpu_custom_call" | custom-call | flops 6553600 | bytes 1327184 | tf_op jit(solution)/shard_map/weights/pallas_call | solution.py:167
  41.5 11.3 %all-to-all-done.1.peaks_ref = f32[32,4,128]{2,1,0:T(4,128)S(1)} async-done(((f32[32,4,128]{2,1,0:T(4,128)}), f32[32,4,128]{2,1,0:T(4,128)S(1)}, u32[]{:S(2)}, u32[]{:S(2)}) %all-to-all-start.1) | async-done | bytes 65568 | tf_op jit(solution)/shard_map/all_to_all | solution.py:179
  52.9 0.0 copy-start.6
  52.9 0.7 copy-done.6
  53.5 0.0 copy-start.2
  53.5 1.0 %copy-done.2 = bf16[512,512]{1,0:T(8,128)(2,1)S(1)} copy-done((bf16[512,512]{1,0:T(8,128)(2,1)S(1)}, bf16[512,512]{1,0:T(8,128)(2,1)}, u32[]{:S(2)}) %copy-start.2) | copy-done | bytes 524312
  54.6 1.3 %project.1 = (f32[16,16,512]{2,1,0:T(8,128)S(1)}, f32[16,16,512]{2,1,0:T(8,128)S(1)}) custom-call(s32[1]{0:T(128)} %bitcast.core_ref, bf16[16,40,512]{2,1,0:T(8,128)(2,1)S(1)} %all_to_all.15.gathered_ref, f32[8,512]{1,0:T(8,128)S(1)} %get-tuple-element.13.smooth_ref, f32[32,4,128]{2,1,0:T(4,128)S(1)} %all-to-all-done.1.peaks_ref, ...), custom_call_target="tpu_custom_call" | custom-call | flops 268435456 | bytes 2310212 | tf_op jit(solution)/shard_map/project/pallas_call | solution.py:167
  55.9 1.9 %collective-permute-start = (f32[16,16,512]{2,1,0:T(8,128)S(1)}, f32[16,16,512]{2,1,0:T(8,128)S(1)}, u32[]{:S(2)}, u32[]{:S(2)}) collective-permute-start(f32[16,16,512]{2,1,0:T(8,128)S(1)} %get-tuple-element.18), channel_id=1, source_target_pairs={{0,16},{16,0},{1,17},{17,1},{2,18},{18,2},{3,19},{19,3},{4,20},{20... | collective-permute-start | bytes 1572872 | tf_op jit(solution)/shard_map/ppermute | solution.py:221
  57.9 1.9 %collective-permute-done.other_ref = f32[16,16,512]{2,1,0:T(8,128)S(1)} collective-permute-done((f32[16,16,512]{2,1,0:T(8,128)S(1)}, f32[16,16,512]{2,1,0:T(8,128)S(1)}, u32[]{:S(2)}, u32[]{:S(2)}) %collective-permute-start) | collective-permute-done | bytes 524320 | tf_op jit(solution)/shard_map/ppermute | solution.py:221
  59.7 0.8 join.1
  60.5 4.8 %all-to-all-start.2 = ((bf16[16,16,512]{2,1,0:T(8,128)(2,1)}), bf16[16,16,512]{2,1,0:T(8,128)(2,1)S(1)}, u32[]{:S(2)}, u32[]{:S(2)}) async-start(bf16[16,16,512]{2,1,0:T(8,128)(2,1)} %join.1), calls=%async_computation.2 | async-start | bytes 524288 | tf_op jit(solution)/shard_map/all_to_all | solution.py:179
  65.3 0.6 copy.8
  65.9 18.2 %all-to-all-done.2.parts_ref = bf16[16,16,512]{2,1,0:T(8,128)(2,1)S(1)} async-done(((bf16[16,16,512]{2,1,0:T(8,128)(2,1)}), bf16[16,16,512]{2,1,0:T(8,128)(2,1)S(1)}, u32[]{:S(2)}, u32[]{:S(2)}) %all-to-all-start.2) | async-done | bytes 262176 | tf_op jit(solution)/shard_map/all_to_all | solution.py:179
  84.1 0.6 sum.1
Async XLA Ops:
  0.6 1.0 %copy-start = (bf16[512,512]{1,0:T(8,128)(2,1)S(1)}, bf16[512,512]{1,0:T(8,128)(2,1)}, u32[]{:S(2)}) copy-start(bf16[512,512]{1,0:T(8,128)(2,1)} %query_ref.3) | copy-start | bytes 1572868
  1.7 0.9 %copy-start.3 = (bf16[512,128]{1,0:T(8,128)(2,1)S(1)}, bf16[512,128]{1,0:T(8,128)(2,1)}, u32[]{:S(2)}) copy-start(bf16[512,128]{1,0:T(8,128)(2,1)} %keyval_ref.3) | copy-start | bytes 393220
  2.6 0.8 copy-start.5
  23.3 16.4 %copy-start.1 = (bf16[512,512]{1,0:T(8,128)(2,1)S(1)}, bf16[512,512]{1,0:T(8,128)(2,1)}, u32[]{:S(2)}) copy-start(bf16[512,512]{1,0:T(8,128)(2,1)} %query_ref.3) | copy-start | bytes 1572868
  24.2 15.5 %copy-start.4 = (bf16[512,128]{1,0:T(8,128)(2,1)S(1)}, bf16[512,128]{1,0:T(8,128)(2,1)}, u32[]{:S(2)}) copy-start(bf16[512,128]{1,0:T(8,128)(2,1)} %keyval_ref.3) | copy-start | bytes 393220
  24.2 28.6 %all-to-all-start.1 = ((f32[32,4,128]{2,1,0:T(4,128)}), f32[32,4,128]{2,1,0:T(4,128)S(1)}, u32[]{:S(2)}, u32[]{:S(2)}) async-start(f32[32,4,128]{2,1,0:T(4,128)} %get-tuple-element.14), calls=%async_computation.1 | async-start | bytes 131072 | tf_op jit(solution)/shard_map/all_to_all | solution.py:179
  52.9 0.7 copy-start.6
  53.5 1.0 %copy-start.2 = (bf16[512,512]{1,0:T(8,128)(2,1)S(1)}, bf16[512,512]{1,0:T(8,128)(2,1)}, u32[]{:S(2)}) copy-start(bf16[512,512]{1,0:T(8,128)(2,1)} %get-tuple-element.22.code_ref) | copy-start | bytes 1572868
  55.9 3.8 %collective-permute-start = (f32[16,16,512]{2,1,0:T(8,128)S(1)}, f32[16,16,512]{2,1,0:T(8,128)S(1)}, u32[]{:S(2)}, u32[]{:S(2)}) collective-permute-start(f32[16,16,512]{2,1,0:T(8,128)S(1)} %get-tuple-element.18), channel_id=1, source_target_pairs={{0,16},{16,0},{1,17},{17,1},{2,18},{18,2},{3,19},{19,3},{4,20},{20... | collective-permute-start | bytes 1572872 | tf_op jit(solution)/shard_map/ppermute | solution.py:221
  60.5 23.6 %all-to-all-start.2 = ((bf16[16,16,512]{2,1,0:T(8,128)(2,1)}), bf16[16,16,512]{2,1,0:T(8,128)(2,1)S(1)}, u32[]{:S(2)}, u32[]{:S(2)}) async-start(bf16[16,16,512]{2,1,0:T(8,128)(2,1)} %join.1), calls=%async_computation.2 | async-start | bytes 524288 | tf_op jit(solution)/shard_map/all_to_all | solution.py:179

commit v3 on v2

v3 whole, which is shorter than its diff:
```python
import functools

import jax
import jax.numpy as jnp
from jax import lax
from jax.experimental import pallas as pl
from jax.experimental.pallas import tpu as pltpu
from jax.sharding import Mesh, PartitionSpec as P

BLOCK = 128
QSTEPS = 4
EPSILON = 1e-06
ROUNDER = 12582912.0
SINE = (
    0.8999999761581421,
    -5.921761989593506,
    11.689058303833008,
    -10.986687660217285,
    6.018372535705566,
    -2.1297717094421387,
    0.45832234621047974,
)
VMEM = pl.BlockSpec(memory_space=pltpu.VMEM)
SMEM = pl.BlockSpec(memory_space=pltpu.SMEM)
HBM = pl.BlockSpec(memory_space=pltpu.HBM)


def soften(value):
    offset = value - ((value + ROUNDER) - ROUNDER)
    square = offset * offset
    series = SINE[-1]
    for term in SINE[-2::-1]:
        series = series * square + term
    return value - offset * series


def across(column_major):
    return jnp.max(column_major.T, axis=0, keepdims=True)


def down(row):
    return jnp.broadcast_to(row, (BLOCK, BLOCK)).T


def peaks_kernel(tokens_hbm, query_hbm, keyval_hbm, out_ref, tokens_ref, query_ref, keyval_ref, sems):
    copies = [
        pltpu.make_async_copy(source, target, sems.at[index])
        for index, (source, target) in enumerate(
            ((query_hbm, query_ref), (keyval_hbm, keyval_ref), (tokens_hbm, tokens_ref))
        )
    ]
    for copy in copies:
        copy.start()
    for copy in copies:
        copy.wait()
    depth = query_ref.shape[0]
    half = tokens_ref.shape[0] // 2
    act = jnp.max(jnp.abs(tokens_ref[...]).astype(jnp.float32), axis=0, keepdims=True)
    peaks = []
    for base in range(0, depth, BLOCK):
        top = jnp.abs(keyval_ref[base : base + BLOCK, :])
        for left in range(0, query_ref.shape[1], BLOCK):
            top = jnp.maximum(top, jnp.abs(query_ref[base : base + BLOCK, left : left + BLOCK]))
        peaks.append(across(top.astype(jnp.float32)))
    weight = jnp.concatenate(peaks, axis=1)
    both = jnp.concatenate(
        [jnp.broadcast_to(act, (4, depth)), jnp.broadcast_to(weight, (4, depth))], axis=0
    ).astype(jnp.bfloat16)
    peers = out_ref.shape[0] // 2
    for core in range(2):
        rows = tokens_ref[core * half : (core + 1) * half, :]
        for peer in range(peers):
            out_ref[core * peers + peer, :half, :] = rows
            out_ref[core * peers + peer, half:, :] = both


def smooth_kernel(gathered_ref, smooth_ref, out_ref):
    members, padded, depth = gathered_ref.shape
    half = padded - 8
    peers = members // 2
    inverses = []
    for core in range(2):
        both = gathered_ref[core * peers, half:, :]
        for peer in range(1, peers):
            both = jnp.maximum(both, gathered_ref[core * peers + peer, half:, :])
        both = both.astype(jnp.float32)
        smooth = jnp.sqrt((both[0:1] + EPSILON) / (both[4:5] + EPSILON))
        smooth_ref[core, 0:1, :] = smooth
        smooth_ref[core, 1:2, :] = 1.0 / smooth
        inverses.append(1.0 / smooth)
    per_block = BLOCK // half
    lines = []
    for first in range(0, peers, per_block):
        top = None
        for core in range(2):
            start = core * peers + first
            for left in range(0, depth, BLOCK):
                piece = jnp.abs(gathered_ref[start : start + per_block, :half, left : left + BLOCK])
                piece = piece.astype(jnp.float32).reshape(BLOCK, BLOCK)
                piece = piece * inverses[core][:, left : left + BLOCK]
                top = piece if top is None else jnp.maximum(top, piece)
        lines.append(across(top))
    peak = jnp.concatenate(lines, axis=0)
    for copy in range(out_ref.shape[0]):
        out_ref[copy] = peak


def weights_kernel(
    core_ref, query_ref, keyval_ref, smooth_ref, send_ref, query_out, query_scale, keyval_out, keyval_scale
):
    smooth = smooth_ref[core_ref[0]][0:1, :]
    depth = query_ref.shape[0]
    lines = []
    for source, code_ref, scale_ref in (
        (query_ref, query_out, query_scale),
        (keyval_ref, keyval_out, keyval_scale),
    ):
        for row, base in enumerate(range(0, depth, BLOCK)):
            factor = down(smooth[:, base : base + BLOCK])
            scales = []
            for column, left in enumerate(range(0, source.shape[1], BLOCK)):
                block = source[base : base + BLOCK, left : left + BLOCK].astype(jnp.float32) * factor
                top = jnp.max(jnp.max(jnp.abs(block), axis=0, keepdims=True), axis=1, keepdims=True)
                scale = (top + EPSILON) / QSTEPS
                scale_ref[row : row + 1, column : column + 1] = scale
                scales.append(jnp.broadcast_to(scale, (1, BLOCK)))
                code = soften(block * (1.0 / scale)).astype(jnp.bfloat16)
                code_ref[base : base + BLOCK, left : left + BLOCK] = code
                if source is query_ref:
                    send_ref[base : base + BLOCK, left : left + BLOCK] = code
            if source is query_ref:
                lines.append(jnp.concatenate(scales, axis=1))
    rest = jnp.concatenate(lines, axis=0)
    pieces = []
    for _ in range(3):
        piece = rest.astype(jnp.bfloat16).astype(jnp.float32)
        rest = rest - piece
        pieces.append(piece)
    pieces.append(jnp.zeros_like(rest))
    send_ref[depth:, :] = jnp.concatenate(pieces, axis=0).astype(jnp.bfloat16)


def project_kernel(core_ref, gathered_ref, smooth_ref, peaks_ref, mine_ref, other_ref, out_ref):
    members, padded, depth = gathered_ref.shape
    half = padded - 8
    peers = members // 2
    peak = peaks_ref[0]
    for member in range(1, peaks_ref.shape[0]):
        peak = jnp.maximum(peak, peaks_ref[member])
    scale = ((peak + EPSILON) / QSTEPS).astype(jnp.bfloat16).astype(jnp.float32)
    per_block = BLOCK // half
    blocks = depth // BLOCK
    sides = []
    for core, code_ref in ((core_ref[0], mine_ref), (1 - core_ref[0], other_ref)):
        pieces = code_ref[depth:, :].astype(jnp.float32)
        column_scale = pieces[0:blocks] + pieces[blocks : 2 * blocks] + pieces[2 * blocks : 3 * blocks]
        sides.append((core * peers, smooth_ref[core][1:2, :], code_ref, column_scale))
    for index, first in enumerate(range(0, peers, per_block)):
        row_scale = down(scale[index : index + 1, :])
        row_inverse = 1.0 / row_scale
        total = None
        for start, inverse, code_ref, column_scale in sides:
            for a in range(blocks):
                left = a * BLOCK
                piece = gathered_ref[pl.ds(start + first, per_block), :half, left : left + BLOCK]
                piece = piece.astype(jnp.float32).reshape(BLOCK, BLOCK)
                value = piece * inverse[:, left : left + BLOCK] * row_inverse
                code = soften(value).astype(jnp.bfloat16)
                product = jnp.dot(
                    code, code_ref[left : left + BLOCK, :], preferred_element_type=jnp.float32
                )
                product = product * column_scale[a : a + 1]
                total = product if total is None else total + product
        width = total.shape[1]
        total = jnp.concatenate(
            [total[:, c : c + BLOCK] * row_scale for c in range(0, width, BLOCK)], axis=1
        )
        out_ref[first : first + per_block] = total.astype(out_ref.dtype).reshape(per_block, half, width)


def sum_kernel(parts_ref, out_ref):
    total = parts_ref[0].astype(jnp.float32)
    for part in range(1, parts_ref.shape[0]):
        total = total + parts_ref[part].astype(jnp.float32)
    out_ref[...] = total.astype(out_ref.dtype)


def call(kernel, out_shape, args, flops=0, specs=None, scratch=(), name=None):
    outs = out_shape if isinstance(out_shape, (tuple, list)) else (out_shape,)
    moved = sum(a.size * a.dtype.itemsize for a in (*args, *outs))
    return pl.pallas_call(
        kernel,
        out_shape=out_shape,
        in_specs=specs or [VMEM] * len(args),
        out_specs=jax.tree.map(lambda _: VMEM, out_shape),
        scratch_shapes=scratch,
        cost_estimate=pl.CostEstimate(flops=flops, bytes_accessed=moved, transcendentals=0),
        compiler_params=pltpu.CompilerParams(vmem_limit_bytes=8 << 20),
        name=name,
    )(*args)


def exchange(array, axes):
    return lax.all_to_all(array, axes, 0, 0, tiled=True)


def body(chips, columns, tokens, query_weight, keyval_weight):
    f32, bf16 = jnp.float32, jnp.bfloat16
    shape = jax.ShapeDtypeStruct
    rows, depth = tokens.shape
    half = rows // 2
    width = query_weight.shape[1]
    blocks = depth // BLOCK
    arguments = (tokens, query_weight, keyval_weight)
    send = call(
        peaks_kernel,
        shape((2 * columns, half + 8, depth), bf16),
        arguments,
        specs=[HBM] * 3,
        scratch=[pltpu.VMEM(a.shape, a.dtype) for a in arguments] + [pltpu.SemaphoreType.DMA((3,))],
        name="peaks",
    )
    gathered = exchange(send, ("core", "y", "x"))
    smooth, row_peaks = call(
        smooth_kernel,
        (shape((2, 8, depth), f32), shape((chips, columns * half // BLOCK, BLOCK), f32)),
        (gathered,),
        name="smooth",
    )
    peaks = exchange(row_peaks, "z")
    core = lax.axis_index("core").astype(jnp.int32).reshape(1)
    mine, query_code, query_scale, keyval_code, keyval_scale = call(
        weights_kernel,
        (
            shape((depth + 4 * blocks, width), bf16),
            shape(query_weight.shape, bf16),
            shape((blocks, width // BLOCK), f32),
            shape(keyval_weight.shape, bf16),
            shape((blocks, keyval_weight.shape[1] // BLOCK), f32),
        ),
        (core, query_weight, keyval_weight, smooth),
        specs=[SMEM] + [VMEM] * 3,
        flops=20 * (query_weight.size + keyval_weight.size),
        name="weights",
    )
    other = lax.ppermute(mine, "core", [(0, 1), (1, 0)])
    partial = call(
        project_kernel,
        shape((chips, half, width), bf16),
        (core, gathered, smooth, peaks, mine, other),
        specs=[SMEM] + [VMEM] * 5,
        flops=2 * columns * rows * depth * width,
        name="project",
    )
    parts = exchange(partial, "z")
    query_proj = call(sum_kernel, shape((half, width), bf16), (parts,), name="sum")
    return (query_proj, query_code, query_scale, keyval_code, keyval_scale)


def solution(mesh):
    rows, columns = mesh.devices.shape
    chips = rows // 2
    side = int(round(columns**0.5))
    fine = Mesh(
        mesh.devices.reshape(chips, 2, columns // side, side), ("z", "core", "y", "x")
    )
    row, col = ("z", "core"), ("y", "x")
    return jax.shard_map(
        functools.partial(body, chips, columns),
        mesh=fine,
        in_specs=(P(col, row), P(row, col), P(row, col)),
        out_specs=(P(row, col),) * 5,
        check_vma=False,
    )
```

time: 85.2 us -> 82.7 us (0.971)
  starting transfers between devices: 22.2 us -> 13.9 us
  blocking collectives: 19.8 us -> 26.2 us
  local copies, waits for them, and re-layouts: 5.02 us -> 3.31 us
    all_to_all x2, starting transfers between devices: 20.3 us -> 12 us  [exchange(): return lax.all_to_all(array, axes, 0, 0, tiled=True)]
    all_to_all x1, blocking collectives: 19.8 us -> 26.2 us  [exchange(): return lax.all_to_all(array, axes, 0, 0, tiled=True)]
    all_to_all x2, waiting for transfers between devices: 29.6 us -> 31.9 us  [exchange(): return lax.all_to_all(array, axes, 0, 0, tiled=True)]
    ppermute x1, waiting for transfers between devices: 1.88 us -> 0.01 us  [body(): other = lax.ppermute(mine, 'core', [(0, 1), (1, 0)])]
    unnamed x15 -> x11, local copies, waits for them, and re-layouts: 5.02 us -> 3.31 us
    pallas_call x6 -> x5, Pallas kernels: 5.61 us -> 6.12 us  [call(): pl.pallas_call(kernel, out_shape=out_shape, in_specs=specs or [VMEM] * le...]
  transfers between devices with their start and end apart: 3 -> 3, of which waited for: 3 -> 2; matrix products, arithmetic and copies ran while one was open for 1% -> 1% of each run, Pallas kernels for 2% -> 0%
where the time goes in v3:
time: 82.7 us; the launch traced here: 82.2 us
  waiting for transfers between devices  31.9 us (39%)
  blocking collectives  26.2 us (32%)
  starting transfers between devices  13.9 us (17%)
  Pallas kernels  6.12 us (7%)
  local copies, waits for them, and re-layouts  3.31 us (4%)
    all_to_all x2, waiting for transfers between devices, exchange(): return lax.all_to_all(array, axes, 0, 0, tiled=True)  31.9 us
    all_to_all x1, blocking collectives, exchange(): return lax.all_to_all(array, axes, 0, 0, tiled=True)  26.2 us
    all_to_all x2, starting transfers between devices, exchange(): return lax.all_to_all(array, axes, 0, 0, tiled=True)  12 us
    pallas_call x5, Pallas kernels, call(): pl.pallas_call(kernel, out_shape=out_shape, in_specs=specs or [VMEM] * le...  6.12 us
    unnamed x11, local copies, waits for them, and re-layouts  3.31 us
    ppermute x1, starting transfers between devices, body(): other = lax.ppermute(mine, 'core', [(0, 1), (1, 0)])  1.91 us
  transfers between devices with their start and end apart: 3, of which 2 were waited for; matrix products, arithmetic and copies ran while one was open for 1% of the time, Pallas kernels for 0%

profile of v3, /device:TPU:32, one launch (start us, length us, event | category | flops | bytes accessed | tf_op | source)
XLA Modules:
  0.0 82.2 jit_solution(1867696934326080797)
XLA Ops:
  0.6 0.0 copy-start
  0.6 1.0 %copy-done = bf16[512,512]{1,0:T(8,128)(2,1)S(1)} copy-done((bf16[512,512]{1,0:T(8,128)(2,1)S(1)}, bf16[512,512]{1,0:T(8,128)(2,1)}, u32[]{:S(2)}) %copy-start) | copy-done | bytes 524312
  1.7 0.0 copy-start.2
  1.7 0.9 %copy-done.2 = bf16[512,128]{1,0:T(8,128)(2,1)S(1)} copy-done((bf16[512,128]{1,0:T(8,128)(2,1)S(1)}, bf16[512,128]{1,0:T(8,128)(2,1)}, u32[]{:S(2)}) %copy-start.2) | copy-done | bytes 131096
  2.6 0.0 copy-start.4
  2.6 0.8 copy-done.4
  3.3 1.4 %peaks.1 = bf16[32,24,512]{2,1,0:T(8,128)(2,1)} custom-call(bf16[32,512]{1,0:T(8,128)(2,1)S(1)} %copy-done.4, bf16[512,512]{1,0:T(8,128)(2,1)S(1)} %copy-done, bf16[512,128]{1,0:T(8,128)(2,1)S(1)} %copy-done.2), custom_call_target="tpu_custom_call" | custom-call | bytes 1474560 | tf_op jit(solution)/shard_map/peaks/pallas_call | solution.py:191
  4.7 7.3 %all-to-all-start = ((bf16[32,24,512]{2,1,0:T(8,128)(2,1)}), bf16[32,24,512]{2,1,0:T(8,128)(2,1)S(1)}, u32[]{:S(2)}, u32[]{:S(2)}) async-start(bf16[32,24,512]{2,1,0:T(8,128)(2,1)} %peaks.1), calls=%async_computation | async-start | bytes 1572864 | tf_op jit(solution)/shard_map/all_to_all | solution.py:204
  12.0 0.0 copy-start.1
  12.1 0.0 copy-start.3
  12.1 14.7 %all-to-all-done.gathered_ref = bf16[32,24,512]{2,1,0:T(8,128)(2,1)S(1)} async-done(((bf16[32,24,512]{2,1,0:T(8,128)(2,1)}), bf16[32,24,512]{2,1,0:T(8,128)(2,1)S(1)}, u32[]{:S(2)}, u32[]{:S(2)}) %all-to-all-start) | async-done | bytes 786464 | tf_op jit(solution)/shard_map/all_to_all | solution.py:204
  26.7 0.2 smooth.1
  27.0 0.0 copy-done.1
  27.0 0.0 copy-done.3
  27.0 1.8 %weights.1 = (bf16[528,512]{1,0:T(8,128)(2,1)S(1)}, bf16[512,512]{1,0:T(8,128)(2,1)}, f32[4,4]{1,0:T(4,128)}, bf16[512,128]{1,0:T(8,128)(2,1)}, f32[4,1]{1,0:T(4,128)S(1)}) custom-call(s32[1]{0:T(128)} %bitcast.core_ref, bf16[512,512]{1,0:T(8,128)(2,1)S(1)} %copy-done.1, bf16[512,128]{1,0:T(8,128)(2,1)S(1)} %copy-done.3, ...), custom_call_target="tpu_custom_call" | custom-call | flops 6553600 | bytes 1884244 | tf_op jit(solution)/shard_map/weights/pallas_call | solution.py:191
  28.8 1.9 %collective-permute-start = (bf16[528,512]{1,0:T(8,128)(2,1)S(1)}, bf16[528,512]{1,0:T(8,128)(2,1)S(1)}, u32[]{:S(2)}, u32[]{:S(2)}) collective-permute-start(bf16[528,512]{1,0:T(8,128)(2,1)S(1)} %get-tuple-element.14.mine_ref), channel_id=1, source_target_pairs={{0,16},{16,0},{1,17},{17,1},{2,18},{18,2},{3,19},{19,3},{4,20},{20... | collective-permute-start | bytes 1622024 | tf_op jit(solution)/shard_map/ppermute | solution.py:246
  30.7 26.2 %all_to_all.15.peaks_ref = f32[16,2,128]{2,1,0:T(2,128)S(1)} all-to-all(f32[16,2,128]{2,1,0:T(2,128)S(1)} %get-tuple-element.13), channel_id=1, replica_groups=mesh['z'=16,'core'=2,'y'=4,'x'=4] {'z'}, dimensions={0} | all-to-all | bytes 32768 | tf_op jit(solution)/shard_map/all_to_all | solution.py:204
  56.9 0.0 collective-permute-done.other_ref
  56.9 2.1 %project.1 = bf16[16,16,512]{2,1,0:T(8,128)(2,1)} custom-call(s32[1]{0:T(128)} %bitcast.core_ref, bf16[32,24,512]{2,1,0:T(8,128)(2,1)S(1)} %all-to-all-done.gathered_ref, f32[2,8,512]{2,1,0:T(8,128)S(1)} %get-tuple-element.12.smooth_ref, f32[16,2,128]{2,1,0:T(2,128)S(1)} %all_to_all.15.peaks_ref, bf16[528,512]{1,0:T(8,128)(2,1)S(1)} %get-tuple-element.14.mine_ref, ...), custom_call_target="tpu_custom_call" | custom-call | flops 268435456 | bytes 2179076 | tf_op jit(solution)/shard_map/project/pallas_call | solution.py:191
  59.0 4.7 %all-to-all-start.2 = ((bf16[16,16,512]{2,1,0:T(8,128)(2,1)}), bf16[16,16,512]{2,1,0:T(8,128)(2,1)S(1)}, u32[]{:S(2)}, u32[]{:S(2)}) async-start(bf16[16,16,512]{2,1,0:T(8,128)(2,1)} %project.1), calls=%async_computation.2 | async-start | bytes 524288 | tf_op jit(solution)/shard_map/all_to_all | solution.py:204
  63.7 0.6 copy.8
  64.3 17.2 %all-to-all-done.2.parts_ref = bf16[16,16,512]{2,1,0:T(8,128)(2,1)S(1)} async-done(((bf16[16,16,512]{2,1,0:T(8,128)(2,1)}), bf16[16,16,512]{2,1,0:T(8,128)(2,1)S(1)}, u32[]{:S(2)}, u32[]{:S(2)}) %all-to-all-start.2) | async-done | bytes 262176 | tf_op jit(solution)/shard_map/all_to_all | solution.py:204
  81.5 0.6 sum.1
Async XLA Ops:
  0.6 1.0 %copy-start = (bf16[512,512]{1,0:T(8,128)(2,1)S(1)}, bf16[512,512]{1,0:T(8,128)(2,1)}, u32[]{:S(2)}) copy-start(bf16[512,512]{1,0:T(8,128)(2,1)} %query_ref.1) | copy-start | bytes 1572868
  1.7 0.9 %copy-start.2 = (bf16[512,128]{1,0:T(8,128)(2,1)S(1)}, bf16[512,128]{1,0:T(8,128)(2,1)}, u32[]{:S(2)}) copy-start(bf16[512,128]{1,0:T(8,128)(2,1)} %keyval_ref.1) | copy-start | bytes 393220
  2.6 0.8 copy-start.4
  4.7 22.0 %all-to-all-start = ((bf16[32,24,512]{2,1,0:T(8,128)(2,1)}), bf16[32,24,512]{2,1,0:T(8,128)(2,1)S(1)}, u32[]{:S(2)}, u32[]{:S(2)}) async-start(bf16[32,24,512]{2,1,0:T(8,128)(2,1)} %peaks.1), calls=%async_computation | async-start | bytes 1572864 | tf_op jit(solution)/shard_map/all_to_all | solution.py:204
  12.0 14.9 %copy-start.1 = (bf16[512,512]{1,0:T(8,128)(2,1)S(1)}, bf16[512,512]{1,0:T(8,128)(2,1)}, u32[]{:S(2)}) copy-start(bf16[512,512]{1,0:T(8,128)(2,1)} %query_ref.1) | copy-start | bytes 1572868
  12.1 14.9 %copy-start.3 = (bf16[512,128]{1,0:T(8,128)(2,1)S(1)}, bf16[512,128]{1,0:T(8,128)(2,1)}, u32[]{:S(2)}) copy-start(bf16[512,128]{1,0:T(8,128)(2,1)} %keyval_ref.1) | copy-start | bytes 393220
  28.8 28.1 %collective-permute-start = (bf16[528,512]{1,0:T(8,128)(2,1)S(1)}, bf16[528,512]{1,0:T(8,128)(2,1)S(1)}, u32[]{:S(2)}, u32[]{:S(2)}) collective-permute-start(bf16[528,512]{1,0:T(8,128)(2,1)S(1)} %get-tuple-element.14.mine_ref), channel_id=1, source_target_pairs={{0,16},{16,0},{1,17},{17,1},{2,18},{18,2},{3,19},{19,3},{4,20},{20... | collective-permute-start | bytes 1622024 | tf_op jit(solution)/shard_map/ppermute | solution.py:246
  59.0 22.5 %all-to-all-start.2 = ((bf16[16,16,512]{2,1,0:T(8,128)(2,1)}), bf16[16,16,512]{2,1,0:T(8,128)(2,1)S(1)}, u32[]{:S(2)}, u32[]{:S(2)}) async-start(bf16[16,16,512]{2,1,0:T(8,128)(2,1)} %project.1), calls=%async_computation.2 | async-start | bytes 524288 | tf_op jit(solution)/shard_map/all_to_all | solution.py:204

commit v4 on v3

--- a/solution.py
+++ b/solution.py
@@ -62,42 +62,47 @@
         for left in range(0, query_ref.shape[1], BLOCK):
             top = jnp.maximum(top, jnp.abs(query_ref[base : base + BLOCK, left : left + BLOCK]))
         peaks.append(across(top.astype(jnp.float32)))
-    weight = jnp.concatenate(peaks, axis=1)
-    both = jnp.concatenate(
-        [jnp.broadcast_to(act, (4, depth)), jnp.broadcast_to(weight, (4, depth))], axis=0
-    ).astype(jnp.bfloat16)
+    acts = [act[:, base : base + BLOCK] for base in range(0, depth, BLOCK)]
+    both = jnp.concatenate(acts + peaks, axis=0).astype(jnp.bfloat16)
     peers = out_ref.shape[0] // 2
     for core in range(2):
-        rows = tokens_ref[core * half : (core + 1) * half, :]
+        for block in range(depth // BLOCK):
+            rows = tokens_ref[core * half : (core + 1) * half, block * BLOCK : (block + 1) * BLOCK]
+            for peer in range(peers):
+                out_ref[core * peers + peer, block * half : (block + 1) * half, :] = rows
         for peer in range(peers):
-            out_ref[core * peers + peer, :half, :] = rows
-            out_ref[core * peers + peer, half:, :] = both
+            out_ref[core * peers + peer, depth // BLOCK * half :, :] = both
 
 
 def smooth_kernel(gathered_ref, smooth_ref, out_ref):
-    members, padded, depth = gathered_ref.shape
-    half = padded - 8
+    members, packed, _ = gathered_ref.shape
+    blocks = smooth_ref.shape[2] // BLOCK
+    half = packed // blocks - 2
     peers = members // 2
     inverses = []
     for core in range(2):
-        both = gathered_ref[core * peers, half:, :]
+        both = gathered_ref[core * peers, blocks * half :, :]
         for peer in range(1, peers):
-            both = jnp.maximum(both, gathered_ref[core * peers + peer, half:, :])
+            both = jnp.maximum(both, gathered_ref[core * peers + peer, blocks * half :, :])
         both = both.astype(jnp.float32)
-        smooth = jnp.sqrt((both[0:1] + EPSILON) / (both[4:5] + EPSILON))
-        smooth_ref[core, 0:1, :] = smooth
-        smooth_ref[core, 1:2, :] = 1.0 / smooth
-        inverses.append(1.0 / smooth)
+        smooth = jnp.sqrt((both[:blocks] + EPSILON) / (both[blocks:] + EPSILON))
+        inverse = 1.0 / smooth
+        for block in range(blocks):
+            lanes = slice(block * BLOCK, (block + 1) * BLOCK)
+            smooth_ref[core, 0:1, lanes] = smooth[block : block + 1]
+            smooth_ref[core, 1:2, lanes] = inverse[block : block + 1]
+        inverses.append(inverse)
     per_block = BLOCK // half
     lines = []
     for first in range(0, peers, per_block):
         top = None
         for core in range(2):
             start = core * peers + first
-            for left in range(0, depth, BLOCK):
-                piece = jnp.abs(gathered_ref[start : start + per_block, :half, left : left + BLOCK])
+            for block in range(blocks):
+                rows = slice(block * half, (block + 1) * half)
+                piece = jnp.abs(gathered_ref[start : start + per_block, rows, :])
                 piece = piece.astype(jnp.float32).reshape(BLOCK, BLOCK)
-                piece = piece * inverses[core][:, left : left + BLOCK]
+                piece = piece * inverses[core][block : block + 1]
                 top = piece if top is None else jnp.maximum(top, piece)
         lines.append(across(top))
     peak = jnp.concatenate(lines, axis=0)
@@ -140,9 +145,10 @@
     send_ref[depth:, :] = jnp.concatenate(pieces, axis=0).astype(jnp.bfloat16)
 
 
-def project_kernel(core_ref, gathered_ref, smooth_ref, peaks_ref, mine_ref, other_ref, out_ref):
-    members, padded, depth = gathered_ref.shape
-    half = padded - 8
+def project_kernel(places, core_ref, gathered_ref, smooth_ref, peaks_ref, mine_ref, other_ref, out_ref):
+    members, _, _ = gathered_ref.shape
+    depth = smooth_ref.shape[2]
+    half = out_ref.shape[1]
     peers = members // 2
     peak = peaks_ref[0]
     for member in range(1, peaks_ref.shape[0]):
@@ -162,7 +168,7 @@
         for start, inverse, code_ref, column_scale in sides:
             for a in range(blocks):
                 left = a * BLOCK
-                piece = gathered_ref[pl.ds(start + first, per_block), :half, left : left + BLOCK]
+                piece = gathered_ref[pl.ds(start + first, per_block), a * half : (a + 1) * half, :]
                 piece = piece.astype(jnp.float32).reshape(BLOCK, BLOCK)
                 value = piece * inverse[:, left : left + BLOCK] * row_inverse
                 code = soften(value).astype(jnp.bfloat16)
@@ -175,7 +181,9 @@
         total = jnp.concatenate(
             [total[:, c : c + BLOCK] * row_scale for c in range(0, width, BLOCK)], axis=1
         )
-        out_ref[first : first + per_block] = total.astype(out_ref.dtype).reshape(per_block, half, width)
+        total = total.astype(out_ref.dtype)
+        for peer in range(per_block):
+            out_ref[places[first + peer]] = total[peer * half : (peer + 1) * half]
 
 
 def sum_kernel(parts_ref, out_ref):
@@ -200,34 +208,37 @@
     )(*args)
 
 
-def exchange(array, axes):
-    return lax.all_to_all(array, axes, 0, 0, tiled=True)
-
-
-def body(chips, columns, tokens, query_weight, keyval_weight):
+def exchange(array, axes, order):
+    return lax.all_to_all(array, axes, 0, 0, tiled=True, axis_index_groups=[order])
+
+
+def body(chips, columns, orders, tokens, query_weight, keyval_weight):
     f32, bf16 = jnp.float32, jnp.bfloat16
     shape = jax.ShapeDtypeStruct
     rows, depth = tokens.shape
     half = rows // 2
     width = query_weight.shape[1]
     blocks = depth // BLOCK
+    chip_order, column_order = orders
+    core_column_order = column_order + [columns + column for column in column_order]
+    places = [chip_order.index(column) for column in column_order]
     arguments = (tokens, query_weight, keyval_weight)
     send = call(
         peaks_kernel,
-        shape((2 * columns, half + 8, depth), bf16),
+        shape((2 * columns, blocks * (half + 2), BLOCK), bf16),
         arguments,
         specs=[HBM] * 3,
         scratch=[pltpu.VMEM(a.shape, a.dtype) for a in arguments] + [pltpu.SemaphoreType.DMA((3,))],
         name="peaks",
     )
-    gathered = exchange(send, ("core", "y", "x"))
+    gathered = exchange(send, ("core", "y", "x"), core_column_order)
     smooth, row_peaks = call(
         smooth_kernel,
         (shape((2, 8, depth), f32), shape((chips, columns * half // BLOCK, BLOCK), f32)),
         (gathered,),
         name="smooth",
     )
-    peaks = exchange(row_peaks, "z")
+    peaks = exchange(row_peaks, "z", chip_order)
     core = lax.axis_index("core").astype(jnp.int32).reshape(1)
     mine, query_code, query_scale, keyval_code, keyval_scale = call(
         weights_kernel,
@@ -245,14 +256,14 @@
     )
     other = lax.ppermute(mine, "core", [(0, 1), (1, 0)])
     partial = call(
-        project_kernel,
+        functools.partial(project_kernel, places),
         shape((chips, half, width), bf16),
         (core, gathered, smooth, peaks, mine, other),
         specs=[SMEM] + [VMEM] * 5,
         flops=2 * columns * rows * depth * width,
         name="project",
     )
-    parts = exchange(partial, "z")
+    parts = exchange(partial, "z", chip_order)
     query_proj = call(sum_kernel, shape((half, width), bf16), (parts,), name="sum")
     return (query_proj, query_code, query_scale, keyval_code, keyval_scale)
 
@@ -260,13 +271,14 @@
 def solution(mesh):
     rows, columns = mesh.devices.shape
     chips = rows // 2
-    side = int(round(columns**0.5))
-    fine = Mesh(
-        mesh.devices.reshape(chips, 2, columns // side, side), ("z", "core", "y", "x")
-    )
+    width = int(round(columns**0.5))
+    height = columns // width
+    fine = Mesh(mesh.devices.reshape(chips, 2, height, width), ("z", "core", "y", "x"))
     row, col = ("z", "core"), ("y", "x")
+    far = lambda size: [(index + size // 2) % size for index in range(size)]
+    orders = (far(chips), [y * width + x for y in far(height) for x in far(width)])
     return jax.shard_map(
-        functools.partial(body, chips, columns),
+        functools.partial(body, chips, columns, orders),
         mesh=fine,
         in_specs=(P(col, row), P(row, col), P(row, col)),
         out_specs=(P(row, col),) * 5,

time: 82.7 us -> 75.4 us (0.912)
  the two profiles are of different devices: /device:TPU:32 before, /device:TPU:1 now
where the time goes in v4:
time: 75.4 us; the launch traced here: 74.9 us
  starting transfers between devices  29 us (38%)
  waiting for transfers between devices  19.1 us (25%)
  blocking collectives  16.8 us (22%)
  Pallas kernels  6.03 us (8%)
  local copies, waits for them, and re-layouts  3.31 us (4%)
    all_to_all x2, starting transfers between devices, exchange(): lax.all_to_all(array, axes, 0, 0, tiled=True, axis_index_groups=[order])  26.8 us
    all_to_all x2, waiting for transfers between devices, exchange(): lax.all_to_all(array, axes, 0, 0, tiled=True, axis_index_groups=[order])  19.1 us
    all_to_all x1, blocking collectives, exchange(): lax.all_to_all(array, axes, 0, 0, tiled=True, axis_index_groups=[order])  16.8 us
    pallas_call x5, Pallas kernels, call(): pl.pallas_call(kernel, out_shape=out_shape, in_specs=specs or [VMEM] * le...  6.03 us
    unnamed x11, local copies, waits for them, and re-layouts  3.31 us
    ppermute x1, starting transfers between devices, body(): other = lax.ppermute(mine, 'core', [(0, 1), (1, 0)])  2.14 us
  transfers between devices with their start and end apart: 3, of which 2 were waited for; matrix products, arithmetic and copies ran while one was open for 1% of the time, Pallas kernels for 0%

profile of v4, /device:TPU:1, one launch (start us, length us, event | category | flops | bytes accessed | tf_op | source)
XLA Modules:
  0.0 74.9 jit_solution(2546110662271277730)
XLA Ops:
  0.6 0.0 copy-start
  0.6 1.0 %copy-done = bf16[512,512]{1,0:T(8,128)(2,1)S(1)} copy-done((bf16[512,512]{1,0:T(8,128)(2,1)S(1)}, bf16[512,512]{1,0:T(8,128)(2,1)}, u32[]{:S(2)}) %copy-start) | copy-done | bytes 524312
  1.7 0.0 copy-start.2
  1.7 0.9 %copy-done.2 = bf16[512,128]{1,0:T(8,128)(2,1)S(1)} copy-done((bf16[512,128]{1,0:T(8,128)(2,1)S(1)}, bf16[512,128]{1,0:T(8,128)(2,1)}, u32[]{:S(2)}) %copy-start.2) | copy-done | bytes 131096
  2.6 0.0 copy-start.4
  2.6 0.8 %copy-done.4 = bf16[32,512]{1,0:T(8,128)(2,1)S(1)} copy-done((bf16[32,512]{1,0:T(8,128)(2,1)S(1)}, bf16[32,512]{1,0:T(8,128)(2,1)}, u32[]{:S(2)}) %copy-start.4) | copy-done | bytes 32792
  3.3 1.3 %peaks.1 = bf16[32,72,128]{2,1,0:T(8,128)(2,1)} custom-call(bf16[32,512]{1,0:T(8,128)(2,1)S(1)} %copy-done.4, bf16[512,512]{1,0:T(8,128)(2,1)S(1)} %copy-done, bf16[512,128]{1,0:T(8,128)(2,1)S(1)} %copy-done.2), custom_call_target="tpu_custom_call" | custom-call | bytes 1277952 | tf_op jit(solution)/shard_map/peaks/pallas_call | solution.py:199
  4.6 0.0 copy-start.3
  4.6 14.0 %all-to-all-start = ((bf16[32,72,128]{2,1,0:T(8,128)(2,1)}), bf16[32,72,128]{2,1,0:T(8,128)(2,1)S(1)}, u32[]{:S(2)}, u32[]{:S(2)}) async-start(bf16[32,72,128]{2,1,0:T(8,128)(2,1)} %peaks.1), calls=%async_computation | async-start | bytes 1179648 | tf_op jit(solution)/shard_map/all_to_all | solution.py:212
  18.7 0.0 copy-start.1
  18.7 7.6 %all-to-all-done.gathered_ref = bf16[32,72,128]{2,1,0:T(8,128)(2,1)S(1)} async-done(((bf16[32,72,128]{2,1,0:T(8,128)(2,1)}), bf16[32,72,128]{2,1,0:T(8,128)(2,1)S(1)}, u32[]{:S(2)}, u32[]{:S(2)}) %all-to-all-start) | async-done | bytes 589856 | tf_op jit(solution)/shard_map/all_to_all | solution.py:212
  26.3 0.2 smooth.1
  26.5 0.0 copy-done.3
  26.5 0.0 copy-done.1
  26.5 1.8 %weights.1 = (bf16[528,512]{1,0:T(8,128)(2,1)S(1)}, bf16[512,512]{1,0:T(8,128)(2,1)}, f32[4,4]{1,0:T(4,128)}, bf16[512,128]{1,0:T(8,128)(2,1)}, f32[4,1]{1,0:T(4,128)S(1)}) custom-call(s32[1]{0:T(128)} %bitcast.core_ref, bf16[512,512]{1,0:T(8,128)(2,1)S(1)} %copy-done.1, bf16[512,128]{1,0:T(8,128)(2,1)S(1)} %copy-done.3, ...), custom_call_target="tpu_custom_call" | custom-call | flops 6553600 | bytes 1884244 | tf_op jit(solution)/shard_map/weights/pallas_call | solution.py:199
  28.3 2.1 %collective-permute-start = (bf16[528,512]{1,0:T(8,128)(2,1)S(1)}, bf16[528,512]{1,0:T(8,128)(2,1)S(1)}, u32[]{:S(2)}, u32[]{:S(2)}) collective-permute-start(bf16[528,512]{1,0:T(8,128)(2,1)S(1)} %get-tuple-element.14.mine_ref), channel_id=1, source_target_pairs={{0,16},{16,0},{1,17},{17,1},{2,18},{18,2},{3,19},{19,3},{4,20},{20... | collective-permute-start | bytes 1622024 | tf_op jit(solution)/shard_map/ppermute | solution.py:257
  30.5 16.8 %all_to_all.15.peaks_ref = f32[16,2,128]{2,1,0:T(2,128)S(1)} all-to-all(f32[16,2,128]{2,1,0:T(2,128)S(1)} %get-tuple-element.13), channel_id=1, replica_groups={{256,288,320,352,384,416,448,480,0,32,64,96,128,160,192,224},{257,289,3..., dimensions={0} | all-to-all | bytes 32768 | tf_op jit(solution)/shard_map/all_to_all | solution.py:212
  47.3 0.0 collective-permute-done.other_ref
  47.3 2.1 %project.1 = bf16[16,16,512]{2,1,0:T(8,128)(2,1)} custom-call(s32[1]{0:T(128)} %bitcast.core_ref, bf16[32,72,128]{2,1,0:T(8,128)(2,1)S(1)} %all-to-all-done.gathered_ref, f32[2,8,512]{2,1,0:T(8,128)S(1)} %get-tuple-element.12.smooth_ref, f32[16,2,128]{2,1,0:T(2,128)S(1)} %all_to_all.15.peaks_ref, bf16[528,512]{1,0:T(8,128)(2,1)S(1)} %get-tuple-element.14.mine_ref, ...), custom_call_target="tpu_custom_call" | custom-call | flops 268435456 | bytes 1982468 | tf_op jit(solution)/shard_map/project/pallas_call | solution.py:199
  49.4 12.8 %all-to-all-start.2 = ((bf16[16,16,512]{2,1,0:T(8,128)(2,1)}), bf16[16,16,512]{2,1,0:T(8,128)(2,1)S(1)}, u32[]{:S(2)}, u32[]{:S(2)}) async-start(bf16[16,16,512]{2,1,0:T(8,128)(2,1)} %project.1), calls=%async_computation.2 | async-start | bytes 524288 | tf_op jit(solution)/shard_map/all_to_all | solution.py:212
  62.2 0.6 copy.8
  62.8 11.5 %all-to-all-done.2.parts_ref = bf16[16,16,512]{2,1,0:T(8,128)(2,1)S(1)} async-done(((bf16[16,16,512]{2,1,0:T(8,128)(2,1)}), bf16[16,16,512]{2,1,0:T(8,128)(2,1)S(1)}, u32[]{:S(2)}, u32[]{:S(2)}) %all-to-all-start.2) | async-done | bytes 262176 | tf_op jit(solution)/shard_map/all_to_all | solution.py:212
  74.2 0.6 sum.1
Async XLA Ops:
  0.6 1.0 %copy-start = (bf16[512,512]{1,0:T(8,128)(2,1)S(1)}, bf16[512,512]{1,0:T(8,128)(2,1)}, u32[]{:S(2)}) copy-start(bf16[512,512]{1,0:T(8,128)(2,1)} %query_ref.1) | copy-start | bytes 1572868
  1.7 0.9 %copy-start.2 = (bf16[512,128]{1,0:T(8,128)(2,1)S(1)}, bf16[512,128]{1,0:T(8,128)(2,1)}, u32[]{:S(2)}) copy-start(bf16[512,128]{1,0:T(8,128)(2,1)} %keyval_ref.1) | copy-start | bytes 393220
  2.6 0.8 %copy-start.4 = (bf16[32,512]{1,0:T(8,128)(2,1)S(1)}, bf16[32,512]{1,0:T(8,128)(2,1)}, u32[]{:S(2)}) copy-start(bf16[32,512]{1,0:T(8,128)(2,1)} %tokens_hbm.1) | copy-start | bytes 98308
  4.6 21.9 %copy-start.3 = (bf16[512,128]{1,0:T(8,128)(2,1)S(1)}, bf16[512,128]{1,0:T(8,128)(2,1)}, u32[]{:S(2)}) copy-start(bf16[512,128]{1,0:T(8,128)(2,1)} %keyval_ref.1) | copy-start | bytes 393220
  4.6 21.6 %all-to-all-start = ((bf16[32,72,128]{2,1,0:T(8,128)(2,1)}), bf16[32,72,128]{2,1,0:T(8,128)(2,1)S(1)}, u32[]{:S(2)}, u32[]{:S(2)}) async-start(bf16[32,72,128]{2,1,0:T(8,128)(2,1)} %peaks.1), calls=%async_computation | async-start | bytes 1179648 | tf_op jit(solution)/shard_map/all_to_all | solution.py:212
  18.7 7.9 %copy-start.1 = (bf16[512,512]{1,0:T(8,128)(2,1)S(1)}, bf16[512,512]{1,0:T(8,128)(2,1)}, u32[]{:S(2)}) copy-start(bf16[512,512]{1,0:T(8,128)(2,1)} %query_ref.1) | copy-start | bytes 1572868
  28.3 19.0 %collective-permute-start = (bf16[528,512]{1,0:T(8,128)(2,1)S(1)}, bf16[528,512]{1,0:T(8,128)(2,1)S(1)}, u32[]{:S(2)}, u32[]{:S(2)}) collective-permute-start(bf16[528,512]{1,0:T(8,128)(2,1)S(1)} %get-tuple-element.14.mine_ref), channel_id=1, source_target_pairs={{0,16},{16,0},{1,17},{17,1},{2,18},{18,2},{3,19},{19,3},{4,20},{20... | collective-permute-start | bytes 1622024 | tf_op jit(solution)/shard_map/ppermute | solution.py:257
  49.4 24.9 %all-to-all-start.2 = ((bf16[16,16,512]{2,1,0:T(8,128)(2,1)}), bf16[16,16,512]{2,1,0:T(8,128)(2,1)S(1)}, u32[]{:S(2)}, u32[]{:S(2)}) async-start(bf16[16,16,512]{2,1,0:T(8,128)(2,1)} %project.1), calls=%async_computation.2 | async-start | bytes 524288 | tf_op jit(solution)/shard_map/all_to_all | solution.py:212

commit v5 on v4

--- a/solution.py
+++ b/solution.py
@@ -6,6 +6,7 @@
 from jax.experimental import pallas as pl
 from jax.experimental.pallas import tpu as pltpu
 from jax.sharding import Mesh, PartitionSpec as P
+
 
 BLOCK = 128
 QSTEPS = 4
@@ -42,7 +43,7 @@
     return jnp.broadcast_to(row, (BLOCK, BLOCK)).T
 
 
-def peaks_kernel(tokens_hbm, query_hbm, keyval_hbm, out_ref, tokens_ref, query_ref, keyval_ref, sems):
+def peaks_kernel(_, tokens_hbm, query_hbm, keyval_hbm, out_ref, tokens_ref, query_ref, keyval_ref, sems):
     copies = [
         pltpu.make_async_copy(source, target, sems.at[index])
         for index, (source, target) in enumerate(
@@ -127,7 +128,10 @@
                 block = source[base : base + BLOCK, left : left + BLOCK].astype(jnp.float32) * factor
                 top = jnp.max(jnp.max(jnp.abs(block), axis=0, keepdims=True), axis=1, keepdims=True)
                 scale = (top + EPSILON) / QSTEPS
-                scale_ref[row : row + 1, column : column + 1] = scale
+                if source is query_ref:
+                    scale_ref[row : row + 1, column : column + 1] = scale
+                else:
+                    scale_ref[column : column + 1, row : row + 1] = scale
                 scales.append(jnp.broadcast_to(scale, (1, BLOCK)))
                 code = soften(block * (1.0 / scale)).astype(jnp.bfloat16)
                 code_ref[base : base + BLOCK, left : left + BLOCK] = code
@@ -193,7 +197,11 @@
     out_ref[...] = total.astype(out_ref.dtype)
 
 
-def call(kernel, out_shape, args, flops=0, specs=None, scratch=(), name=None):
+def call(kernel, out_shape, args, **options):
+    return launch(kernel, out_shape, args, **options)
+
+
+def launch(kernel, out_shape, args, flops=0, specs=None, scratch=()):
     outs = out_shape if isinstance(out_shape, (tuple, list)) else (out_shape,)
     moved = sum(a.size * a.dtype.itemsize for a in (*args, *outs))
     return pl.pallas_call(
@@ -204,7 +212,6 @@
         scratch_shapes=scratch,
         cost_estimate=pl.CostEstimate(flops=flops, bytes_accessed=moved, transcendentals=0),
         compiler_params=pltpu.CompilerParams(vmem_limit_bytes=8 << 20),
-        name=name,
     )(*args)
 
 
@@ -223,23 +230,21 @@
     core_column_order = column_order + [columns + column for column in column_order]
     places = [chip_order.index(column) for column in column_order]
     arguments = (tokens, query_weight, keyval_weight)
+    core = lax.axis_index("core").astype(jnp.int32).reshape(1)
     send = call(
         peaks_kernel,
         shape((2 * columns, blocks * (half + 2), BLOCK), bf16),
-        arguments,
-        specs=[HBM] * 3,
+        (core, *(pltpu.with_memory_space_constraint(a, pltpu.HBM) for a in arguments)),
+        specs=[SMEM] + [HBM] * 3,
         scratch=[pltpu.VMEM(a.shape, a.dtype) for a in arguments] + [pltpu.SemaphoreType.DMA((3,))],
-        name="peaks",
     )
     gathered = exchange(send, ("core", "y", "x"), core_column_order)
     smooth, row_peaks = call(
         smooth_kernel,
         (shape((2, 8, depth), f32), shape((chips, columns * half // BLOCK, BLOCK), f32)),
         (gathered,),
-        name="smooth",
     )
     peaks = exchange(row_peaks, "z", chip_order)
-    core = lax.axis_index("core").astype(jnp.int32).reshape(1)
     mine, query_code, query_scale, keyval_code, keyval_scale = call(
         weights_kernel,
         (
@@ -247,12 +252,11 @@
             shape(query_weight.shape, bf16),
             shape((blocks, width // BLOCK), f32),
             shape(keyval_weight.shape, bf16),
-            shape((blocks, keyval_weight.shape[1] // BLOCK), f32),
+            shape((keyval_weight.shape[1] // BLOCK, blocks), f32),
         ),
         (core, query_weight, keyval_weight, smooth),
         specs=[SMEM] + [VMEM] * 3,
         flops=20 * (query_weight.size + keyval_weight.size),
-        name="weights",
     )
     other = lax.ppermute(mine, "core", [(0, 1), (1, 0)])
     partial = call(
@@ -261,11 +265,10 @@
         (core, gathered, smooth, peaks, mine, other),
         specs=[SMEM] + [VMEM] * 5,
         flops=2 * columns * rows * depth * width,
-        name="project",
     )
     parts = exchange(partial, "z", chip_order)
-    query_proj = call(sum_kernel, shape((half, width), bf16), (parts,), name="sum")
-    return (query_proj, query_code, query_scale, keyval_code, keyval_scale)
+    query_proj = call(sum_kernel, shape((half, width), bf16), (parts,))
+    return (query_proj, query_code, query_scale, keyval_code, keyval_scale.T)
 
 
 def solution(mesh):

time: 75.4 us -> 71.1 us (0.943)
  the two profiles are of different devices: /device:TPU:1 before, /device:TPU:6 now
where the time goes in v5:
time: 71.1 us; the launch traced here: 70.8 us
  blocking collectives  62 us (87%)
  Pallas kernels  5.39 us (8%)
  starting transfers between devices  1.91 us (3%)
  local copies, waits for them, and re-layouts  0.8 us (1%)
    all_to_all x3, blocking collectives, exchange(): lax.all_to_all(array, axes, 0, 0, tiled=True, axis_index_groups=[order])  62 us
    pallas_call x5, Pallas kernels, launch(): pl.pallas_call(kernel, out_shape=out_shape, in_specs=specs or [VMEM] * le...  5.39 us
    ppermute x1, starting transfers between devices, body(): other = lax.ppermute(mine, 'core', [(0, 1), (1, 0)])  1.91 us
  transfers between devices with their start and end apart: 1, of which 0 were waited for; matrix products, arithmetic and copies ran while one was open for 0% of the time, Pallas kernels for 0%

profile of v5, /device:TPU:6, one launch (start us, length us, event | category | flops | bytes accessed | tf_op | source)
XLA Modules:
  0.0 70.8 jit_solution(17033646318606409856)
XLA Ops:
  0.6 1.3 %shard_map.74 = bf16[32,72,128]{2,1,0:T(8,128)(2,1)S(1)} custom-call(s32[1]{0:T(128)} %bitcast._.core_ref, bf16[32,512]{1,0:T(8,128)(2,1)} %tokens_hbm.1, bf16[512,512]{1,0:T(8,128)(2,1)} %query_ref.1, bf16[512,128]{1,0:T(8,128)(2,1)} %keyval_ref.1), custom_call_target="tpu_custom_call" | custom-call | bytes 1277956 | tf_op jit(solution)/shard_map/pallas_call | solution.py:207
  2.0 0.0 copy-start.1
  2.0 20.3 %all_to_all.15.gathered_ref = bf16[32,72,128]{2,1,0:T(8,128)(2,1)S(1)} all-to-all(bf16[32,72,128]{2,1,0:T(8,128)(2,1)S(1)} %shard_map.74), channel_id=1, replica_groups={{10,11,8,9,14,15,12,13,2,3,0,1,6,7,4,5,26,27,24,25,30,31,28,29,18,19,16..., dimensions={0} | all-to-all | bytes 1179648 | tf_op jit(solution)/shard_map/all_to_all | solution.py:219
  22.3 0.0 copy-start
  22.3 0.2 shard_map.75
  22.6 0.0 copy-done.1
  22.6 0.8 %copy-done = bf16[512,512]{1,0:T(8,128)(2,1)S(1)} copy-done((bf16[512,512]{1,0:T(8,128)(2,1)S(1)}, bf16[512,512]{1,0:T(8,128)(2,1)}, u32[]{:S(2)}) %copy-start) | copy-done | bytes 524312
  23.4 1.8 %shard_map.76 = (bf16[528,512]{1,0:T(8,128)(2,1)S(1)}, bf16[512,512]{1,0:T(8,128)(2,1)}, f32[4,4]{1,0:T(4,128)}, bf16[512,128]{1,0:T(8,128)(2,1)}, f32[1,4]{1,0:T(1,128)}) custom-call(s32[1]{0:T(128)} %bitcast._.core_ref, bf16[512,512]{1,0:T(8,128)(2,1)S(1)} %copy-done, bf16[512,128]{1,0:T(8,128)(2,1)S(1)} %copy-done.1, ...), custom_call_target="tpu_custom_call" | custom-call | flops 6553600 | bytes 1884244 | tf_op jit(solution)/shard_map/pallas_call | solution.py:207
  25.2 1.9 %collective-permute-start = (bf16[528,512]{1,0:T(8,128)(2,1)S(1)}, bf16[528,512]{1,0:T(8,128)(2,1)S(1)}, u32[]{:S(2)}, u32[]{:S(2)}) collective-permute-start(bf16[528,512]{1,0:T(8,128)(2,1)S(1)} %get-tuple-element.14.mine_ref), channel_id=1, source_target_pairs={{0,16},{16,0},{1,17},{17,1},{2,18},{18,2},{3,19},{19,3},{4,20},{20... | collective-permute-start | bytes 1622024 | tf_op jit(solution)/shard_map/ppermute | solution.py:261
  27.1 17.6 %all_to_all.16.peaks_ref = f32[16,2,128]{2,1,0:T(2,128)S(1)} all-to-all(f32[16,2,128]{2,1,0:T(2,128)S(1)} %get-tuple-element.13), channel_id=1, replica_groups={{256,288,320,352,384,416,448,480,0,32,64,96,128,160,192,224},{257,289,3..., dimensions={0} | all-to-all | bytes 32768 | tf_op jit(solution)/shard_map/all_to_all | solution.py:219
  44.7 0.0 collective-permute-done.other_ref
  44.7 1.4 %shard_map.77 = bf16[16,16,512]{2,1,0:T(8,128)(2,1)S(1)} custom-call(s32[1]{0:T(128)} %bitcast._.core_ref, bf16[32,72,128]{2,1,0:T(8,128)(2,1)S(1)} %all_to_all.15.gathered_ref, f32[2,8,512]{2,1,0:T(8,128)S(1)} %get-tuple-element.12.smooth_ref, f32[16,2,128]{2,1,0:T(2,128)S(1)} %all_to_all.16.peaks_ref, bf16[528,512]{1,0:T(8,128)(2,1)S(1)} %get-tuple-element.14.mine_ref, ...), custom_call_target="tpu_custom_call" | custom-call | flops 268435456 | bytes 1982468 | tf_op jit(solution)/shard_map/pallas_call | solution.py:207
  46.1 24.1 %all_to_all.17.parts_ref = bf16[16,16,512]{2,1,0:T(8,128)(2,1)S(1)} all-to-all(bf16[16,16,512]{2,1,0:T(8,128)(2,1)S(1)} %shard_map.77), channel_id=1, replica_groups={{256,288,320,352,384,416,448,480,0,32,64,96,128,160,192,224},{257,289,3..., dimensions={0} | all-to-all | bytes 524288 | tf_op jit(solution)/shard_map/all_to_all | solution.py:219
  70.2 0.6 shard_map.78
Async XLA Ops:
  2.0 20.6 %copy-start.1 = (bf16[512,128]{1,0:T(8,128)(2,1)S(1)}, bf16[512,128]{1,0:T(8,128)(2,1)}, u32[]{:S(2)}) copy-start(bf16[512,128]{1,0:T(8,128)(2,1)} %keyval_ref.1) | copy-start | bytes 393220
  22.3 1.0 %copy-start = (bf16[512,512]{1,0:T(8,128)(2,1)S(1)}, bf16[512,512]{1,0:T(8,128)(2,1)}, u32[]{:S(2)}) copy-start(bf16[512,512]{1,0:T(8,128)(2,1)} %query_ref.1) | copy-start | bytes 1572868
  25.2 19.5 %collective-permute-start = (bf16[528,512]{1,0:T(8,128)(2,1)S(1)}, bf16[528,512]{1,0:T(8,128)(2,1)S(1)}, u32[]{:S(2)}, u32[]{:S(2)}) collective-permute-start(bf16[528,512]{1,0:T(8,128)(2,1)S(1)} %get-tuple-element.14.mine_ref), channel_id=1, source_target_pairs={{0,16},{16,0},{1,17},{17,1},{2,18},{18,2},{3,19},{19,3},{4,20},{20... | collective-permute-start | bytes 1622024 | tf_op jit(solution)/shard_map/ppermute | solution.py:261

commit v6 on v5

--- a/solution.py
+++ b/solution.py
@@ -111,45 +111,35 @@
         out_ref[copy] = peak
 
 
-def weights_kernel(
-    core_ref, query_ref, keyval_ref, smooth_ref, send_ref, query_out, query_scale, keyval_out, keyval_scale
-):
-    smooth = smooth_ref[core_ref[0]][0:1, :]
-    depth = query_ref.shape[0]
-    lines = []
-    for source, code_ref, scale_ref in (
-        (query_ref, query_out, query_scale),
-        (keyval_ref, keyval_out, keyval_scale),
+def encode(core, query_ref, other_ref, keyval_ref, smooth_ref, outs):
+    query_out, query_scale, mine_out, mine_scale, other_out, other_scale, keyval_out, keyval_scale = outs
+    for source, side, targets in (
+        (query_ref, core, ((query_out, query_scale), (mine_out, mine_scale))),
+        (other_ref, 1 - core, ((other_out, other_scale),)),
+        (keyval_ref, core, ((keyval_out, keyval_scale),)),
     ):
-        for row, base in enumerate(range(0, depth, BLOCK)):
+        smooth = smooth_ref[side][0:1, :]
+        for row, base in enumerate(range(0, source.shape[0], BLOCK)):
             factor = down(smooth[:, base : base + BLOCK])
-            scales = []
             for column, left in enumerate(range(0, source.shape[1], BLOCK)):
                 block = source[base : base + BLOCK, left : left + BLOCK].astype(jnp.float32) * factor
                 top = jnp.max(jnp.max(jnp.abs(block), axis=0, keepdims=True), axis=1, keepdims=True)
                 scale = (top + EPSILON) / QSTEPS
-                if source is query_ref:
-                    scale_ref[row : row + 1, column : column + 1] = scale
-                else:
-                    scale_ref[column : column + 1, row : row + 1] = scale
-                scales.append(jnp.broadcast_to(scale, (1, BLOCK)))
                 code = soften(block * (1.0 / scale)).astype(jnp.bfloat16)
-                code_ref[base : base + BLOCK, left : left + BLOCK] = code
-                if source is query_ref:
-                    send_ref[base : base + BLOCK, left : left + BLOCK] = code
-            if source is query_ref:
-                lines.append(jnp.concatenate(scales, axis=1))
-    rest = jnp.concatenate(lines, axis=0)
-    pieces = []
-    for _ in range(3):
-        piece = rest.astype(jnp.bfloat16).astype(jnp.float32)
-        rest = rest - piece
-        pieces.append(piece)
-    pieces.append(jnp.zeros_like(rest))
-    send_ref[depth:, :] = jnp.concatenate(pieces, axis=0).astype(jnp.bfloat16)
-
-
-def project_kernel(places, core_ref, gathered_ref, smooth_ref, peaks_ref, mine_ref, other_ref, out_ref):
+                for code_ref, scale_ref in targets:
+                    if source is keyval_ref:
+                        scale_ref[column : column + 1, row : row + 1] = scale
+                    else:
+                        scale_ref[row : row + 1, column : column + 1] = scale
+                    code_ref[base : base + BLOCK, left : left + BLOCK] = code
+
+
+def weights_kernel(core_ref, query_ref, other_ref, keyval_ref, smooth_ref, *outs):
+    encode(core_ref[0], query_ref, other_ref, keyval_ref, smooth_ref, outs)
+
+
+def project_kernel(places, core_ref, gathered_ref, smooth_ref, peaks_ref, *refs):
+    mine_ref, mine_scale, other_ref, other_scale, out_ref = refs
     members, _, _ = gathered_ref.shape
     depth = smooth_ref.shape[2]
     half = out_ref.shape[1]
@@ -161,9 +151,20 @@
     per_block = BLOCK // half
     blocks = depth // BLOCK
     sides = []
-    for core, code_ref in ((core_ref[0], mine_ref), (1 - core_ref[0], other_ref)):
-        pieces = code_ref[depth:, :].astype(jnp.float32)
-        column_scale = pieces[0:blocks] + pieces[blocks : 2 * blocks] + pieces[2 * blocks : 3 * blocks]
+    for core, code_ref, scale_ref in (
+        (core_ref[0], mine_ref, mine_scale),
+        (1 - core_ref[0], other_ref, other_scale),
+    ):
+        column_scale = [
+            jnp.concatenate(
+                [
+                    jnp.broadcast_to(scale_ref[a : a + 1, c : c + 1], (1, BLOCK))
+                    for c in range(scale_ref.shape[1])
+                ],
+                axis=1,
+            )
+            for a in range(blocks)
+        ]
         sides.append((core * peers, smooth_ref[core][1:2, :], code_ref, column_scale))
     for index, first in enumerate(range(0, peers, per_block)):
         row_scale = down(scale[index : index + 1, :])
@@ -179,7 +180,7 @@
                 product = jnp.dot(
                     code, code_ref[left : left + BLOCK, :], preferred_element_type=jnp.float32
                 )
-                product = product * column_scale[a : a + 1]
+                product = product * column_scale[a]
                 total = product if total is None else total + product
         width = total.shape[1]
         total = jnp.concatenate(
@@ -226,9 +227,9 @@
     half = rows // 2
     width = query_weight.shape[1]
     blocks = depth // BLOCK
-    chip_order, column_order = orders
+    peak_order, part_order, column_order = orders
     core_column_order = column_order + [columns + column for column in column_order]
-    places = [chip_order.index(column) for column in column_order]
+    places = [part_order.index(column) for column in column_order]
     arguments = (tokens, query_weight, keyval_weight)
     core = lax.axis_index("core").astype(jnp.int32).reshape(1)
     send = call(
@@ -239,34 +240,34 @@
         scratch=[pltpu.VMEM(a.shape, a.dtype) for a in arguments] + [pltpu.SemaphoreType.DMA((3,))],
     )
     gathered = exchange(send, ("core", "y", "x"), core_column_order)
+    other_weight = lax.ppermute(query_weight, "core", [(0, 1), (1, 0)])
     smooth, row_peaks = call(
         smooth_kernel,
         (shape((2, 8, depth), f32), shape((chips, columns * half // BLOCK, BLOCK), f32)),
         (gathered,),
     )
-    peaks = exchange(row_peaks, "z", chip_order)
-    mine, query_code, query_scale, keyval_code, keyval_scale = call(
+    peaks = exchange(row_peaks, "z", peak_order)
+    code = shape(query_weight.shape, bf16)
+    scale = shape((blocks, width // BLOCK), f32)
+    query_code, query_scale, *both, keyval_code, keyval_scale = call(
         weights_kernel,
         (
-            shape((depth + 4 * blocks, width), bf16),
-            shape(query_weight.shape, bf16),
-            shape((blocks, width // BLOCK), f32),
+            *(code, scale) * 3,
             shape(keyval_weight.shape, bf16),
             shape((keyval_weight.shape[1] // BLOCK, blocks), f32),
         ),
-        (core, query_weight, keyval_weight, smooth),
-        specs=[SMEM] + [VMEM] * 3,
-        flops=20 * (query_weight.size + keyval_weight.size),
-    )
-    other = lax.ppermute(mine, "core", [(0, 1), (1, 0)])
+        (core, query_weight, other_weight, keyval_weight, smooth),
+        specs=[SMEM] + [VMEM] * 4,
+        flops=20 * (2 * query_weight.size + keyval_weight.size),
+    )
     partial = call(
         functools.partial(project_kernel, places),
         shape((chips, half, width), bf16),
-        (core, gathered, smooth, peaks, mine, other),
-        specs=[SMEM] + [VMEM] * 5,
+        (core, gathered, smooth, peaks, *both),
+        specs=[SMEM] + [VMEM] * 7,
         flops=2 * columns * rows * depth * width,
     )
-    parts = exchange(partial, "z", chip_order)
+    parts = exchange(partial, "z", part_order)
     query_proj = call(sum_kernel, shape((half, width), bf16), (parts,))
     return (query_proj, query_code, query_scale, keyval_code, keyval_scale.T)
 
@@ -278,8 +279,12 @@
     height = columns // width
     fine = Mesh(mesh.devices.reshape(chips, 2, height, width), ("z", "core", "y", "x"))
     row, col = ("z", "core"), ("y", "x")
-    far = lambda size: [(index + size // 2) % size for index in range(size)]
-    orders = (far(chips), [y * width + x for y in far(height) for x in far(width)])
+    turned = lambda size, first: [(index + first) % size for index in range(size)]
+    orders = (
+        turned(chips, 11 * chips // 16),
+        turned(chips, chips // 2),
+        [y * width + x for y in turned(height, height - 1) for x in turned(width, width - 1)],
+    )
     return jax.shard_map(
         functools.partial(body, chips, columns, orders),
         mesh=fine,

time: 71.1 us -> 67.4 us (0.948)
  the two profiles are of different devices: /device:TPU:6 before, /device:TPU:8 now
where the time goes in v6:
time: 67.4 us; the launch traced here: 67.1 us
  starting transfers between devices  26.6 us (39%)
  blocking collectives  22.9 us (34%)
  waiting for transfers between devices  9.3 us (14%)
  Pallas kernels  7.54 us (11%)
  between operations  0.7 us (1%)
    all_to_all x2, starting transfers between devices, exchange(): lax.all_to_all(array, axes, 0, 0, tiled=True, axis_index_groups=[order])  24.4 us
    all_to_all x1, blocking collectives, exchange(): lax.all_to_all(array, axes, 0, 0, tiled=True, axis_index_groups=[order])  22.9 us
    all_to_all x2, waiting for transfers between devices, exchange(): lax.all_to_all(array, axes, 0, 0, tiled=True, axis_index_groups=[order])  9.29 us
    pallas_call x5, Pallas kernels, launch(): pl.pallas_call(kernel, out_shape=out_shape, in_specs=specs or [VMEM] * le...  7.54 us
    ppermute x1, starting transfers between devices, body(): other_weight = lax.ppermute(query_weight, 'core', [(0, 1), (1, 0)])  2.2 us
  transfers between devices with their start and end apart: 3, of which 2 were waited for; matrix products, arithmetic and copies ran while one was open for 0% of the time, Pallas kernels for 5%

profile of v6, /device:TPU:8, one launch (start us, length us, event | category | flops | bytes accessed | tf_op | source)
XLA Modules:
  0.0 67.1 jit_solution(12442030169196637474)
XLA Ops:
  0.6 2.1 %shard_map.74 = bf16[32,72,128]{2,1,0:T(8,128)(2,1)} custom-call(s32[1]{0:T(128)} %bitcast._.core_ref, bf16[32,512]{1,0:T(8,128)(2,1)} %tokens_hbm.1, bf16[512,512]{1,0:T(8,128)(2,1)} %query_ref.1, bf16[512,128]{1,0:T(8,128)(2,1)} %keyval_ref.1), custom_call_target="tpu_custom_call" | custom-call | bytes 1277956 | tf_op jit(solution)/shard_map/pallas_call | solution.py:208
  2.8 0.0 copy-start
  2.8 11.6 %all-to-all-start = ((bf16[32,72,128]{2,1,0:T(8,128)(2,1)}), bf16[32,72,128]{2,1,0:T(8,128)(2,1)S(1)}, u32[]{:S(2)}, u32[]{:S(2)}) async-start(bf16[32,72,128]{2,1,0:T(8,128)(2,1)} %shard_map.74), calls=%async_computation | async-start | bytes 1179648 | tf_op jit(solution)/shard_map/all_to_all | solution.py:220
  14.3 0.0 copy-done
  14.3 0.0 copy-start.1
  14.4 2.2 %collective-permute-start = (bf16[512,512]{1,0:T(8,128)(2,1)S(1)}, bf16[512,512]{1,0:T(8,128)(2,1)S(1)}, u32[]{:S(2)}, u32[]{:S(2)}) collective-permute-start(bf16[512,512]{1,0:T(8,128)(2,1)S(1)} %copy-done), channel_id=1, source_target_pairs={{0,16},{16,0},{1,17},{17,1},{2,18},{18,2},{3,19},{19,3},{4,20},{20... | collective-permute-start | bytes 1572872 | tf_op jit(solution)/shard_map/ppermute | solution.py:243
  16.6 6.7 %all-to-all-done.gathered_ref = bf16[32,72,128]{2,1,0:T(8,128)(2,1)S(1)} async-done(((bf16[32,72,128]{2,1,0:T(8,128)(2,1)}), bf16[32,72,128]{2,1,0:T(8,128)(2,1)S(1)}, u32[]{:S(2)}, u32[]{:S(2)}) %all-to-all-start) | async-done | bytes 589856 | tf_op jit(solution)/shard_map/all_to_all | solution.py:220
  23.3 0.8 %shard_map.75 = (f32[2,8,512]{2,1,0:T(8,128)S(1)}, f32[16,2,128]{2,1,0:T(2,128)}) custom-call(bf16[32,72,128]{2,1,0:T(8,128)(2,1)S(1)} %all-to-all-done.gathered_ref), custom_call_target="tpu_custom_call" | custom-call | bytes 638976 | tf_op jit(solution)/shard_map/pallas_call | solution.py:208
  24.1 12.9 %all-to-all-start.1 = ((f32[16,2,128]{2,1,0:T(2,128)}), f32[16,2,128]{2,1,0:T(2,128)S(1)}, u32[]{:S(2)}, u32[]{:S(2)}) async-start(f32[16,2,128]{2,1,0:T(2,128)} %get-tuple-element.16), calls=%async_computation.1 | async-start | bytes 32768 | tf_op jit(solution)/shard_map/all_to_all | solution.py:220
  37.0 0.0 collective-permute-done.other_ref
  37.0 0.0 copy-done.1
  37.0 2.7 %shard_map.76 = (bf16[512,512]{1,0:T(8,128)(2,1)}, f32[4,4]{1,0:T(4,128)}, bf16[512,512]{1,0:T(8,128)(2,1)S(1)}, f32[4,4]{1,0:T(4,128)S(1)}, bf16[512,512]{1,0:T...) custom-call(s32[1]{0:T(128)} %bitcast._.core_ref, bf16[512,512]{1,0:T(8,128)(2,1)S(1)} %copy-done, ...), custom_call_target="tpu_custom_call" | custom-call | flops 11796480 | bytes 2916564 | tf_op jit(solution)/shard_map/pallas_call | solution.py:208
  39.7 2.6 %all-to-all-done.1.peaks_ref = f32[16,2,128]{2,1,0:T(2,128)S(1)} async-done(((f32[16,2,128]{2,1,0:T(2,128)}), f32[16,2,128]{2,1,0:T(2,128)S(1)}, u32[]{:S(2)}, u32[]{:S(2)}) %all-to-all-start.1) | async-done | bytes 16416 | tf_op jit(solution)/shard_map/all_to_all | solution.py:220
  42.3 1.3 %shard_map.77 = bf16[16,16,512]{2,1,0:T(8,128)(2,1)S(1)} custom-call(s32[1]{0:T(128)} %bitcast._.core_ref, bf16[32,72,128]{2,1,0:T(8,128)(2,1)S(1)} %all-to-all-done.gathered_ref, f32[2,8,512]{2,1,0:T(8,128)S(1)} %get-tuple-element.15.smooth_ref, f32[16,2,128]{2,1,0:T(2,128)S(1)} %all-to-all-done.1.peaks_ref, ...), custom_call_target="tpu_custom_call" | custom-call | flops 268435456 | bytes 1949828 | tf_op jit(solution)/shard_map/pallas_call | solution.py:208
  43.5 22.9 %all_to_all.15.parts_ref = bf16[16,16,512]{2,1,0:T(8,128)(2,1)S(1)} all-to-all(bf16[16,16,512]{2,1,0:T(8,128)(2,1)S(1)} %shard_map.77), channel_id=1, replica_groups={{256,288,320,352,384,416,448,480,0,32,64,96,128,160,192,224},{257,289,3..., dimensions={0} | all-to-all | bytes 524288 | tf_op jit(solution)/shard_map/all_to_all | solution.py:220
  66.4 0.6 shard_map.78
Async XLA Ops:
  2.8 11.6 %copy-start = (bf16[512,512]{1,0:T(8,128)(2,1)S(1)}, bf16[512,512]{1,0:T(8,128)(2,1)}, u32[]{:S(2)}) copy-start(bf16[512,512]{1,0:T(8,128)(2,1)} %query_ref.1) | copy-start | bytes 1572868
  2.8 20.5 %all-to-all-start = ((bf16[32,72,128]{2,1,0:T(8,128)(2,1)}), bf16[32,72,128]{2,1,0:T(8,128)(2,1)S(1)}, u32[]{:S(2)}, u32[]{:S(2)}) async-start(bf16[32,72,128]{2,1,0:T(8,128)(2,1)} %shard_map.74), calls=%async_computation | async-start | bytes 1179648 | tf_op jit(solution)/shard_map/all_to_all | solution.py:220
  14.3 22.7 %copy-start.1 = (bf16[512,128]{1,0:T(8,128)(2,1)S(1)}, bf16[512,128]{1,0:T(8,128)(2,1)}, u32[]{:S(2)}) copy-start(bf16[512,128]{1,0:T(8,128)(2,1)} %keyval_ref.1) | copy-start | bytes 393220
  14.4 22.6 %collective-permute-start = (bf16[512,512]{1,0:T(8,128)(2,1)S(1)}, bf16[512,512]{1,0:T(8,128)(2,1)S(1)}, u32[]{:S(2)}, u32[]{:S(2)}) collective-permute-start(bf16[512,512]{1,0:T(8,128)(2,1)S(1)} %copy-done), channel_id=1, source_target_pairs={{0,16},{16,0},{1,17},{17,1},{2,18},{18,2},{3,19},{19,3},{4,20},{20... | collective-permute-start | bytes 1572872 | tf_op jit(solution)/shard_map/ppermute | solution.py:243
  24.1 18.1 %all-to-all-start.1 = ((f32[16,2,128]{2,1,0:T(2,128)}), f32[16,2,128]{2,1,0:T(2,128)S(1)}, u32[]{:S(2)}, u32[]{:S(2)}) async-start(f32[16,2,128]{2,1,0:T(2,128)} %get-tuple-element.16), calls=%async_computation.1 | async-start | bytes 32768 | tf_op jit(solution)/shard_map/all_to_all | solution.py:220

commit v7 on v6

--- a/solution.py
+++ b/solution.py
@@ -280,9 +280,12 @@
     fine = Mesh(mesh.devices.reshape(chips, 2, height, width), ("z", "core", "y", "x"))
     row, col = ("z", "core"), ("y", "x")
     turned = lambda size, first: [(index + first) % size for index in range(size)]
+    facing = lambda size, first: [
+        (first + index + side * size // 2) % size for index in range(size // 2) for side in range(2)
+    ]
     orders = (
-        turned(chips, 11 * chips // 16),
-        turned(chips, chips // 2),
+        facing(chips, 11 * chips // 16),
+        facing(chips, chips // 2),
         [y * width + x for y in turned(height, height - 1) for x in turned(width, width - 1)],
     )
     return jax.shard_map(

time: 67.4 us -> 66.3 us (0.984)
  the two profiles are of different devices: /device:TPU:8 before, /device:TPU:32 now
where the time goes in v7:
time: 66.3 us; the launch traced here: 65.9 us
  starting transfers between devices  26.9 us (41%)
  blocking collectives  22.3 us (34%)
  waiting for transfers between devices  8.55 us (13%)
  Pallas kernels  7.54 us (11%)
  between operations  0.7 us (1%)
    all_to_all x2, starting transfers between devices, exchange(): lax.all_to_all(array, axes, 0, 0, tiled=True, axis_index_groups=[order])  24.6 us
    all_to_all x1, blocking collectives, exchange(): lax.all_to_all(array, axes, 0, 0, tiled=True, axis_index_groups=[order])  22.3 us
    all_to_all x2, waiting for transfers between devices, exchange(): lax.all_to_all(array, axes, 0, 0, tiled=True, axis_index_groups=[order])  8.55 us
    pallas_call x5, Pallas kernels, launch(): pl.pallas_call(kernel, out_shape=out_shape, in_specs=specs or [VMEM] * le...  7.54 us
    ppermute x1, starting transfers between devices, body(): other_weight = lax.ppermute(query_weight, 'core', [(0, 1), (1, 0)])  2.26 us
  transfers between devices with their start and end apart: 3, of which 2 were waited for; matrix products, arithmetic and copies ran while one was open for 0% of the time, Pallas kernels for 5%

profile of v7, /device:TPU:32, one launch (start us, length us, event | category | flops | bytes accessed | tf_op | source)
XLA Modules:
  0.0 65.9 jit_solution(9945490637502354950)
XLA Ops:
  0.6 2.1 %shard_map.74 = bf16[32,72,128]{2,1,0:T(8,128)(2,1)} custom-call(s32[1]{0:T(128)} %bitcast._.core_ref, bf16[32,512]{1,0:T(8,128)(2,1)} %tokens_hbm.1, bf16[512,512]{1,0:T(8,128)(2,1)} %query_ref.1, bf16[512,128]{1,0:T(8,128)(2,1)} %keyval_ref.1), custom_call_target="tpu_custom_call" | custom-call | bytes 1277956 | tf_op jit(solution)/shard_map/pallas_call | solution.py:208
  2.8 0.0 copy-start
  2.8 8.9 %all-to-all-start = ((bf16[32,72,128]{2,1,0:T(8,128)(2,1)}), bf16[32,72,128]{2,1,0:T(8,128)(2,1)S(1)}, u32[]{:S(2)}, u32[]{:S(2)}) async-start(bf16[32,72,128]{2,1,0:T(8,128)(2,1)} %shard_map.74), calls=%async_computation | async-start | bytes 1179648 | tf_op jit(solution)/shard_map/all_to_all | solution.py:220
  11.7 0.0 copy-done
  11.7 0.0 copy-start.1
  11.7 2.3 %collective-permute-start = (bf16[512,512]{1,0:T(8,128)(2,1)S(1)}, bf16[512,512]{1,0:T(8,128)(2,1)S(1)}, u32[]{:S(2)}, u32[]{:S(2)}) collective-permute-start(bf16[512,512]{1,0:T(8,128)(2,1)S(1)} %copy-done), channel_id=1, source_target_pairs={{0,16},{16,0},{1,17},{17,1},{2,18},{18,2},{3,19},{19,3},{4,20},{20... | collective-permute-start | bytes 1572872 | tf_op jit(solution)/shard_map/ppermute | solution.py:243
  14.0 6.8 %all-to-all-done.gathered_ref = bf16[32,72,128]{2,1,0:T(8,128)(2,1)S(1)} async-done(((bf16[32,72,128]{2,1,0:T(8,128)(2,1)}), bf16[32,72,128]{2,1,0:T(8,128)(2,1)S(1)}, u32[]{:S(2)}, u32[]{:S(2)}) %all-to-all-start) | async-done | bytes 589856 | tf_op jit(solution)/shard_map/all_to_all | solution.py:220
  20.8 0.8 %shard_map.75 = (f32[2,8,512]{2,1,0:T(8,128)S(1)}, f32[16,2,128]{2,1,0:T(2,128)}) custom-call(bf16[32,72,128]{2,1,0:T(8,128)(2,1)S(1)} %all-to-all-done.gathered_ref), custom_call_target="tpu_custom_call" | custom-call | bytes 638976 | tf_op jit(solution)/shard_map/pallas_call | solution.py:208
  21.6 15.7 %all-to-all-start.1 = ((f32[16,2,128]{2,1,0:T(2,128)}), f32[16,2,128]{2,1,0:T(2,128)S(1)}, u32[]{:S(2)}, u32[]{:S(2)}) async-start(f32[16,2,128]{2,1,0:T(2,128)} %get-tuple-element.16), calls=%async_computation.1 | async-start | bytes 32768 | tf_op jit(solution)/shard_map/all_to_all | solution.py:220
  37.3 0.0 collective-permute-done.other_ref
  37.4 0.0 copy-done.1
  37.4 2.7 %shard_map.76 = (bf16[512,512]{1,0:T(8,128)(2,1)}, f32[4,4]{1,0:T(4,128)}, bf16[512,512]{1,0:T(8,128)(2,1)S(1)}, f32[4,4]{1,0:T(4,128)S(1)}, bf16[512,512]{1,0:T...) custom-call(s32[1]{0:T(128)} %bitcast._.core_ref, bf16[512,512]{1,0:T(8,128)(2,1)S(1)} %copy-done, ...), custom_call_target="tpu_custom_call" | custom-call | flops 11796480 | bytes 2916564 | tf_op jit(solution)/shard_map/pallas_call | solution.py:208
  40.0 1.8 %all-to-all-done.1.peaks_ref = f32[16,2,128]{2,1,0:T(2,128)S(1)} async-done(((f32[16,2,128]{2,1,0:T(2,128)}), f32[16,2,128]{2,1,0:T(2,128)S(1)}, u32[]{:S(2)}, u32[]{:S(2)}) %all-to-all-start.1) | async-done | bytes 16416 | tf_op jit(solution)/shard_map/all_to_all | solution.py:220
  41.8 1.3 %shard_map.77 = bf16[16,16,512]{2,1,0:T(8,128)(2,1)S(1)} custom-call(s32[1]{0:T(128)} %bitcast._.core_ref, bf16[32,72,128]{2,1,0:T(8,128)(2,1)S(1)} %all-to-all-done.gathered_ref, f32[2,8,512]{2,1,0:T(8,128)S(1)} %get-tuple-element.15.smooth_ref, f32[16,2,128]{2,1,0:T(2,128)S(1)} %all-to-all-done.1.peaks_ref, ...), custom_call_target="tpu_custom_call" | custom-call | flops 268435456 | bytes 1949828 | tf_op jit(solution)/shard_map/pallas_call | solution.py:208
  43.0 22.3 %all_to_all.15.parts_ref = bf16[16,16,512]{2,1,0:T(8,128)(2,1)S(1)} all-to-all(bf16[16,16,512]{2,1,0:T(8,128)(2,1)S(1)} %shard_map.77), channel_id=1, replica_groups={{256,0,288,32,320,64,352,96,384,128,416,160,448,192,480,224},{257,1,289..., dimensions={0} | all-to-all | bytes 524288 | tf_op jit(solution)/shard_map/all_to_all | solution.py:220
  65.3 0.6 shard_map.78
Async XLA Ops:
  2.8 8.9 %copy-start = (bf16[512,512]{1,0:T(8,128)(2,1)S(1)}, bf16[512,512]{1,0:T(8,128)(2,1)}, u32[]{:S(2)}) copy-start(bf16[512,512]{1,0:T(8,128)(2,1)} %query_ref.1) | copy-start | bytes 1572868
  2.8 18.0 %all-to-all-start = ((bf16[32,72,128]{2,1,0:T(8,128)(2,1)}), bf16[32,72,128]{2,1,0:T(8,128)(2,1)S(1)}, u32[]{:S(2)}, u32[]{:S(2)}) async-start(bf16[32,72,128]{2,1,0:T(8,128)(2,1)} %shard_map.74), calls=%async_computation | async-start | bytes 1179648 | tf_op jit(solution)/shard_map/all_to_all | solution.py:220
  11.7 25.6 %copy-start.1 = (bf16[512,128]{1,0:T(8,128)(2,1)S(1)}, bf16[512,128]{1,0:T(8,128)(2,1)}, u32[]{:S(2)}) copy-start(bf16[512,128]{1,0:T(8,128)(2,1)} %keyval_ref.1) | copy-start | bytes 393220
  11.7 25.6 %collective-permute-start = (bf16[512,512]{1,0:T(8,128)(2,1)S(1)}, bf16[512,512]{1,0:T(8,128)(2,1)S(1)}, u32[]{:S(2)}, u32[]{:S(2)}) collective-permute-start(bf16[512,512]{1,0:T(8,128)(2,1)S(1)} %copy-done), channel_id=1, source_target_pairs={{0,16},{16,0},{1,17},{17,1},{2,18},{18,2},{3,19},{19,3},{4,20},{20... | collective-permute-start | bytes 1572872 | tf_op jit(solution)/shard_map/ppermute | solution.py:243
  21.6 20.1 %all-to-all-start.1 = ((f32[16,2,128]{2,1,0:T(2,128)}), f32[16,2,128]{2,1,0:T(2,128)S(1)}, u32[]{:S(2)}, u32[]{:S(2)}) async-start(f32[16,2,128]{2,1,0:T(2,128)} %get-tuple-element.16), calls=%async_computation.1 | async-start | bytes 32768 | tf_op jit(solution)/shard_map/all_to_all | solution.py:220

commit v8 on v7

--- a/solution.py
+++ b/solution.py
@@ -43,36 +43,47 @@
     return jnp.broadcast_to(row, (BLOCK, BLOCK)).T
 
 
-def peaks_kernel(_, tokens_hbm, query_hbm, keyval_hbm, out_ref, tokens_ref, query_ref, keyval_ref, sems):
-    copies = [
-        pltpu.make_async_copy(source, target, sems.at[index])
+def peaks_kernel(_, tokens_hbm, query_hbm, keyval_hbm, out_hbm, *scratch):
+    tokens_ref, query_ref, keyval_ref, rows_ref, both_ref, load_sems, send_sems = scratch
+    loads = [
+        pltpu.make_async_copy(source, target, load_sems.at[index])
         for index, (source, target) in enumerate(
-            ((query_hbm, query_ref), (keyval_hbm, keyval_ref), (tokens_hbm, tokens_ref))
+            ((tokens_hbm, tokens_ref), (query_hbm, query_ref), (keyval_hbm, keyval_ref))
         )
     ]
-    for copy in copies:
-        copy.start()
-    for copy in copies:
-        copy.wait()
+    for load in loads:
+        load.start()
     depth = query_ref.shape[0]
     half = tokens_ref.shape[0] // 2
+    body = depth // BLOCK * half
+    members = out_hbm.shape[0]
+    loads[0].wait()
+    for core in range(2):
+        for block in range(depth // BLOCK):
+            rows = tokens_ref[core * half : (core + 1) * half, block * BLOCK : (block + 1) * BLOCK]
+            for peer in range(members // 2):
+                rows_ref[(1 - core) * members // 2 + peer, block * half : (block + 1) * half, :] = rows
+    sends = [
+        pltpu.make_async_copy(rows_ref, out_hbm.at[:, pl.ds(0, body), :], send_sems.at[0]),
+        pltpu.make_async_copy(both_ref, out_hbm.at[:, pl.ds(body, both_ref.shape[1]), :], send_sems.at[1]),
+    ]
+    sends[0].start()
     act = jnp.max(jnp.abs(tokens_ref[...]).astype(jnp.float32), axis=0, keepdims=True)
+    acts = [act[:, base : base + BLOCK] for base in range(0, depth, BLOCK)]
+    loads[1].wait()
+    loads[2].wait()
     peaks = []
     for base in range(0, depth, BLOCK):
         top = jnp.abs(keyval_ref[base : base + BLOCK, :])
         for left in range(0, query_ref.shape[1], BLOCK):
             top = jnp.maximum(top, jnp.abs(query_ref[base : base + BLOCK, left : left + BLOCK]))
         peaks.append(across(top.astype(jnp.float32)))
-    acts = [act[:, base : base + BLOCK] for base in range(0, depth, BLOCK)]
     both = jnp.concatenate(acts + peaks, axis=0).astype(jnp.bfloat16)
-    peers = out_ref.shape[0] // 2
-    for core in range(2):
-        for block in range(depth // BLOCK):
-            rows = tokens_ref[core * half : (core + 1) * half, block * BLOCK : (block + 1) * BLOCK]
-            for peer in range(peers):
-                out_ref[core * peers + peer, block * half : (block + 1) * half, :] = rows
-        for peer in range(peers):
-            out_ref[core * peers + peer, depth // BLOCK * half :, :] = both
+    for member in range(members):
+        both_ref[member] = both
+    sends[1].start()
+    for send in sends:
+        send.wait()
 
 
 def smooth_kernel(gathered_ref, smooth_ref, out_ref):
@@ -82,9 +93,9 @@
     peers = members // 2
     inverses = []
     for core in range(2):
-        both = gathered_ref[core * peers, blocks * half :, :]
+        both = gathered_ref[(1 - core) * peers, blocks * half :, :]
         for peer in range(1, peers):
-            both = jnp.maximum(both, gathered_ref[core * peers + peer, blocks * half :, :])
+            both = jnp.maximum(both, gathered_ref[(1 - core) * peers + peer, blocks * half :, :])
         both = both.astype(jnp.float32)
         smooth = jnp.sqrt((both[:blocks] + EPSILON) / (both[blocks:] + EPSILON))
         inverse = 1.0 / smooth
@@ -98,7 +109,7 @@
     for first in range(0, peers, per_block):
         top = None
         for core in range(2):
-            start = core * peers + first
+            start = (1 - core) * peers + first
             for block in range(blocks):
                 rows = slice(block * half, (block + 1) * half)
                 piece = jnp.abs(gathered_ref[start : start + per_block, rows, :])
@@ -165,7 +176,7 @@
             )
             for a in range(blocks)
         ]
-        sides.append((core * peers, smooth_ref[core][1:2, :], code_ref, column_scale))
+        sides.append(((1 - core) * peers, smooth_ref[core][1:2, :], code_ref, column_scale))
     for index, first in enumerate(range(0, peers, per_block)):
         row_scale = down(scale[index : index + 1, :])
         row_inverse = 1.0 / row_scale
@@ -202,14 +213,14 @@
     return launch(kernel, out_shape, args, **options)
 
 
-def launch(kernel, out_shape, args, flops=0, specs=None, scratch=()):
+def launch(kernel, out_shape, args, flops=0, specs=None, out_specs=None, scratch=()):
     outs = out_shape if isinstance(out_shape, (tuple, list)) else (out_shape,)
     moved = sum(a.size * a.dtype.itemsize for a in (*args, *outs))
     return pl.pallas_call(
         kernel,
         out_shape=out_shape,
         in_specs=specs or [VMEM] * len(args),
-        out_specs=jax.tree.map(lambda _: VMEM, out_shape),
+        out_specs=out_specs or jax.tree.map(lambda _: VMEM, out_shape),
         scratch_shapes=scratch,
         cost_estimate=pl.CostEstimate(flops=flops, bytes_accessed=moved, transcendentals=0),
         compiler_params=pltpu.CompilerParams(vmem_limit_bytes=8 << 20),
@@ -228,7 +239,7 @@
     width = query_weight.shape[1]
     blocks = depth // BLOCK
     peak_order, part_order, column_order = orders
-    core_column_order = column_order + [columns + column for column in column_order]
+    core_column_order = [columns + column for column in column_order] + column_order
     places = [part_order.index(column) for column in column_order]
     arguments = (tokens, query_weight, keyval_weight)
     core = lax.axis_index("core").astype(jnp.int32).reshape(1)
@@ -237,7 +248,14 @@
         shape((2 * columns, blocks * (half + 2), BLOCK), bf16),
         (core, *(pltpu.with_memory_space_constraint(a, pltpu.HBM) for a in arguments)),
         specs=[SMEM] + [HBM] * 3,
-        scratch=[pltpu.VMEM(a.shape, a.dtype) for a in arguments] + [pltpu.SemaphoreType.DMA((3,))],
+        out_specs=HBM,
+        scratch=[
+            *(pltpu.VMEM(a.shape, a.dtype) for a in arguments),
+            pltpu.VMEM((2 * columns, blocks * half, BLOCK), bf16),
+            pltpu.VMEM((2 * columns, 2 * blocks, BLOCK), bf16),
+            pltpu.SemaphoreType.DMA((3,)),
+            pltpu.SemaphoreType.DMA((2,)),
+        ],
     )
     gathered = exchange(send, ("core", "y", "x"), core_column_order)
     other_weight = lax.ppermute(query_weight, "core", [(0, 1), (1, 0)])
@@ -283,9 +301,12 @@
     facing = lambda size, first: [
         (first + index + side * size // 2) % size for index in range(size // 2) for side in range(2)
     ]
+    apart = lambda size, first: [
+        member for index in range(size - first) for member in (first + index, index)
+    ] + [first - 1, size - first]
     orders = (
-        facing(chips, 11 * chips // 16),
-        facing(chips, chips // 2),
+        facing(chips, 5 * chips // 8),
+        apart(chips, chips // 2 + 1),
         [y * width + x for y in turned(height, height - 1) for x in turned(width, width - 1)],
     )
     return jax.shard_map(

time: 66.3 us -> 65.7 us (level)
  the two profiles are of different devices: /device:TPU:32 before, /device:TPU:1 now
where the time goes in v8:
time: 65.7 us; the launch traced here: 65.3 us
  starting transfers between devices  28.6 us (44%)
  blocking collectives  22 us (33%)
  Pallas kernels  7.38 us (11%)
  waiting for transfers between devices  6.58 us (10%)
  between operations  0.7 us (1%)
    all_to_all x2, starting transfers between devices, exchange(): lax.all_to_all(array, axes, 0, 0, tiled=True, axis_index_groups=[order])  26.2 us
    all_to_all x1, blocking collectives, exchange(): lax.all_to_all(array, axes, 0, 0, tiled=True, axis_index_groups=[order])  22 us
    pallas_call x5, Pallas kernels, launch(): pl.pallas_call(kernel, out_shape=out_shape, in_specs=specs or [VMEM] * le...  7.38 us
    all_to_all x2, waiting for transfers between devices, exchange(): lax.all_to_all(array, axes, 0, 0, tiled=True, axis_index_groups=[order])  6.58 us
    ppermute x1, starting transfers between devices, body(): other_weight = lax.ppermute(query_weight, 'core', [(0, 1), (1, 0)])  2.46 us
  transfers between devices with their start and end apart: 3, of which 2 were waited for; matrix products, arithmetic and copies ran while one was open for 0% of the time, Pallas kernels for 5%

profile of v8, /device:TPU:1, one launch (start us, length us, event | category | flops | bytes accessed | tf_op | source)
XLA Modules:
  0.0 65.3 jit_solution(8888778103055452616)
XLA Ops:
  0.6 2.0 %shard_map.74 = bf16[32,72,128]{2,1,0:T(8,128)(2,1)} custom-call(s32[1]{0:T(128)} %bitcast._.core_ref, bf16[32,512]{1,0:T(8,128)(2,1)} %tokens_hbm.1, bf16[512,512]{1,0:T(8,128)(2,1)} %query_ref.1, bf16[512,128]{1,0:T(8,128)(2,1)} %keyval_ref.1), custom_call_target="tpu_custom_call" | custom-call | bytes 1277956 | tf_op jit(solution)/shard_map/pallas_call | solution.py:219
  2.6 0.0 copy-start
  2.6 13.1 %all-to-all-start = ((bf16[32,72,128]{2,1,0:T(8,128)(2,1)}), bf16[32,72,128]{2,1,0:T(8,128)(2,1)S(1)}, u32[]{:S(2)}, u32[]{:S(2)}) async-start(bf16[32,72,128]{2,1,0:T(8,128)(2,1)} %shard_map.74), calls=%async_computation | async-start | bytes 1179648 | tf_op jit(solution)/shard_map/all_to_all | solution.py:231
  15.7 0.0 copy-done
  15.7 0.0 copy-start.1
  15.7 2.5 %collective-permute-start = (bf16[512,512]{1,0:T(8,128)(2,1)S(1)}, bf16[512,512]{1,0:T(8,128)(2,1)S(1)}, u32[]{:S(2)}, u32[]{:S(2)}) collective-permute-start(bf16[512,512]{1,0:T(8,128)(2,1)S(1)} %copy-done), channel_id=1, source_target_pairs={{0,16},{16,0},{1,17},{17,1},{2,18},{18,2},{3,19},{19,3},{4,20},{20... | collective-permute-start | bytes 1572872 | tf_op jit(solution)/shard_map/ppermute | solution.py:261
  18.2 5.7 %all-to-all-done.gathered_ref = bf16[32,72,128]{2,1,0:T(8,128)(2,1)S(1)} async-done(((bf16[32,72,128]{2,1,0:T(8,128)(2,1)}), bf16[32,72,128]{2,1,0:T(8,128)(2,1)S(1)}, u32[]{:S(2)}, u32[]{:S(2)}) %all-to-all-start) | async-done | bytes 589856 | tf_op jit(solution)/shard_map/all_to_all | solution.py:231
  23.9 0.8 %shard_map.75 = (f32[2,8,512]{2,1,0:T(8,128)S(1)}, f32[16,2,128]{2,1,0:T(2,128)}) custom-call(bf16[32,72,128]{2,1,0:T(8,128)(2,1)S(1)} %all-to-all-done.gathered_ref), custom_call_target="tpu_custom_call" | custom-call | bytes 638976 | tf_op jit(solution)/shard_map/pallas_call | solution.py:219
  24.7 13.1 %all-to-all-start.1 = ((f32[16,2,128]{2,1,0:T(2,128)}), f32[16,2,128]{2,1,0:T(2,128)S(1)}, u32[]{:S(2)}, u32[]{:S(2)}) async-start(f32[16,2,128]{2,1,0:T(2,128)} %get-tuple-element.16), calls=%async_computation.1 | async-start | bytes 32768 | tf_op jit(solution)/shard_map/all_to_all | solution.py:231
  37.8 0.0 collective-permute-done.other_ref
  37.8 0.0 copy-done.1
  37.8 2.7 %shard_map.76 = (bf16[512,512]{1,0:T(8,128)(2,1)}, f32[4,4]{1,0:T(4,128)}, bf16[512,512]{1,0:T(8,128)(2,1)S(1)}, f32[4,4]{1,0:T(4,128)S(1)}, bf16[512,512]{1,0:T...) custom-call(s32[1]{0:T(128)} %bitcast._.core_ref, bf16[512,512]{1,0:T(8,128)(2,1)S(1)} %copy-done, ...), custom_call_target="tpu_custom_call" | custom-call | flops 11796480 | bytes 2916564 | tf_op jit(solution)/shard_map/pallas_call | solution.py:219
  40.5 0.9 %all-to-all-done.1.peaks_ref = f32[16,2,128]{2,1,0:T(2,128)S(1)} async-done(((f32[16,2,128]{2,1,0:T(2,128)}), f32[16,2,128]{2,1,0:T(2,128)S(1)}, u32[]{:S(2)}, u32[]{:S(2)}) %all-to-all-start.1) | async-done | bytes 16416 | tf_op jit(solution)/shard_map/all_to_all | solution.py:231
  41.4 1.3 %shard_map.77 = bf16[16,16,512]{2,1,0:T(8,128)(2,1)S(1)} custom-call(s32[1]{0:T(128)} %bitcast._.core_ref, bf16[32,72,128]{2,1,0:T(8,128)(2,1)S(1)} %all-to-all-done.gathered_ref, f32[2,8,512]{2,1,0:T(8,128)S(1)} %get-tuple-element.15.smooth_ref, f32[16,2,128]{2,1,0:T(2,128)S(1)} %all-to-all-done.1.peaks_ref, ...), custom_call_target="tpu_custom_call" | custom-call | flops 268435456 | bytes 1949828 | tf_op jit(solution)/shard_map/pallas_call | solution.py:219
  42.7 22.0 %all_to_all.15.parts_ref = bf16[16,16,512]{2,1,0:T(8,128)(2,1)S(1)} all-to-all(bf16[16,16,512]{2,1,0:T(8,128)(2,1)S(1)} %shard_map.77), channel_id=1, replica_groups={{288,0,320,32,352,64,384,96,416,128,448,160,480,192,256,224},{289,1,321..., dimensions={0} | all-to-all | bytes 524288 | tf_op jit(solution)/shard_map/all_to_all | solution.py:231
  64.7 0.6 shard_map.78
Async XLA Ops:
  2.6 13.1 %copy-start = (bf16[512,512]{1,0:T(8,128)(2,1)S(1)}, bf16[512,512]{1,0:T(8,128)(2,1)}, u32[]{:S(2)}) copy-start(bf16[512,512]{1,0:T(8,128)(2,1)} %query_ref.1) | copy-start | bytes 1572868
  2.6 21.2 %all-to-all-start = ((bf16[32,72,128]{2,1,0:T(8,128)(2,1)}), bf16[32,72,128]{2,1,0:T(8,128)(2,1)S(1)}, u32[]{:S(2)}, u32[]{:S(2)}) async-start(bf16[32,72,128]{2,1,0:T(8,128)(2,1)} %shard_map.74), calls=%async_computation | async-start | bytes 1179648 | tf_op jit(solution)/shard_map/all_to_all | solution.py:231
  15.7 22.1 %copy-start.1 = (bf16[512,128]{1,0:T(8,128)(2,1)S(1)}, bf16[512,128]{1,0:T(8,128)(2,1)}, u32[]{:S(2)}) copy-start(bf16[512,128]{1,0:T(8,128)(2,1)} %keyval_ref.1) | copy-start | bytes 393220
  15.7 22.1 %collective-permute-start = (bf16[512,512]{1,0:T(8,128)(2,1)S(1)}, bf16[512,512]{1,0:T(8,128)(2,1)S(1)}, u32[]{:S(2)}, u32[]{:S(2)}) collective-permute-start(bf16[512,512]{1,0:T(8,128)(2,1)S(1)} %copy-done), channel_id=1, source_target_pairs={{0,16},{16,0},{1,17},{17,1},{2,18},{18,2},{3,19},{19,3},{4,20},{20... | collective-permute-start | bytes 1572872 | tf_op jit(solution)/shard_map/ppermute | solution.py:261
  24.7 16.7 %all-to-all-start.1 = ((f32[16,2,128]{2,1,0:T(2,128)}), f32[16,2,128]{2,1,0:T(2,128)S(1)}, u32[]{:S(2)}, u32[]{:S(2)}) async-start(f32[16,2,128]{2,1,0:T(2,128)} %get-tuple-element.16), calls=%async_computation.1 | async-start | bytes 32768 | tf_op jit(solution)/shard_map/all_to_all | solution.py:231

commit v9 on v8

--- a/solution.py
+++ b/solution.py
@@ -301,12 +301,9 @@
     facing = lambda size, first: [
         (first + index + side * size // 2) % size for index in range(size // 2) for side in range(2)
     ]
-    apart = lambda size, first: [
-        member for index in range(size - first) for member in (first + index, index)
-    ] + [first - 1, size - first]
     orders = (
         facing(chips, 5 * chips // 8),
-        apart(chips, chips // 2 + 1),
+        facing(chips, chips // 2),
         [y * width + x for y in turned(height, height - 1) for x in turned(width, width - 1)],
     )
     return jax.shard_map(

time: 65.7 us -> 65.6 us (level)
  the two profiles are of different devices: /device:TPU:1 before, /device:TPU:32 now
where the time goes in v9:
time: 65.6 us; the launch traced here: 65.3 us
  starting transfers between devices  27.3 us (42%)
  blocking collectives  22.2 us (34%)
  waiting for transfers between devices  7.62 us (12%)
  Pallas kernels  7.38 us (11%)
  between operations  0.7 us (1%)
    all_to_all x2, starting transfers between devices, exchange(): lax.all_to_all(array, axes, 0, 0, tiled=True, axis_index_groups=[order])  25.2 us
    all_to_all x1, blocking collectives, exchange(): lax.all_to_all(array, axes, 0, 0, tiled=True, axis_index_groups=[order])  22.2 us
    all_to_all x2, waiting for transfers between devices, exchange(): lax.all_to_all(array, axes, 0, 0, tiled=True, axis_index_groups=[order])  7.61 us
    pallas_call x5, Pallas kernels, launch(): pl.pallas_call(kernel, out_shape=out_shape, in_specs=specs or [VMEM] * le...  7.38 us
    ppermute x1, starting transfers between devices, body(): other_weight = lax.ppermute(query_weight, 'core', [(0, 1), (1, 0)])  2.13 us
  transfers between devices with their start and end apart: 3, of which 2 were waited for; matrix products, arithmetic and copies ran while one was open for 0% of the time, Pallas kernels for 5%

profile of v9, /device:TPU:32, one launch (start us, length us, event | category | flops | bytes accessed | tf_op | source)
XLA Modules:
  0.0 65.3 jit_solution(13738085239166904477)
XLA Ops:
  0.6 2.0 %shard_map.74 = bf16[32,72,128]{2,1,0:T(8,128)(2,1)} custom-call(s32[1]{0:T(128)} %bitcast._.core_ref, bf16[32,512]{1,0:T(8,128)(2,1)} %tokens_hbm.1, bf16[512,512]{1,0:T(8,128)(2,1)} %query_ref.1, bf16[512,128]{1,0:T(8,128)(2,1)} %keyval_ref.1), custom_call_target="tpu_custom_call" | custom-call | bytes 1277956 | tf_op jit(solution)/shard_map/pallas_call | solution.py:219
  2.6 0.0 copy-start
  2.6 8.6 %all-to-all-start = ((bf16[32,72,128]{2,1,0:T(8,128)(2,1)}), bf16[32,72,128]{2,1,0:T(8,128)(2,1)S(1)}, u32[]{:S(2)}, u32[]{:S(2)}) async-start(bf16[32,72,128]{2,1,0:T(8,128)(2,1)} %shard_map.74), calls=%async_computation | async-start | bytes 1179648 | tf_op jit(solution)/shard_map/all_to_all | solution.py:231
  11.2 0.0 copy-done
  11.2 0.0 copy-start.1
  11.2 2.1 %collective-permute-start = (bf16[512,512]{1,0:T(8,128)(2,1)S(1)}, bf16[512,512]{1,0:T(8,128)(2,1)S(1)}, u32[]{:S(2)}, u32[]{:S(2)}) collective-permute-start(bf16[512,512]{1,0:T(8,128)(2,1)S(1)} %copy-done), channel_id=1, source_target_pairs={{0,16},{16,0},{1,17},{17,1},{2,18},{18,2},{3,19},{19,3},{4,20},{20... | collective-permute-start | bytes 1572872 | tf_op jit(solution)/shard_map/ppermute | solution.py:261
  13.4 6.8 %all-to-all-done.gathered_ref = bf16[32,72,128]{2,1,0:T(8,128)(2,1)S(1)} async-done(((bf16[32,72,128]{2,1,0:T(8,128)(2,1)}), bf16[32,72,128]{2,1,0:T(8,128)(2,1)S(1)}, u32[]{:S(2)}, u32[]{:S(2)}) %all-to-all-start) | async-done | bytes 589856 | tf_op jit(solution)/shard_map/all_to_all | solution.py:231
  20.1 0.8 %shard_map.75 = (f32[2,8,512]{2,1,0:T(8,128)S(1)}, f32[16,2,128]{2,1,0:T(2,128)}) custom-call(bf16[32,72,128]{2,1,0:T(8,128)(2,1)S(1)} %all-to-all-done.gathered_ref), custom_call_target="tpu_custom_call" | custom-call | bytes 638976 | tf_op jit(solution)/shard_map/pallas_call | solution.py:219
  21.0 16.6 %all-to-all-start.1 = ((f32[16,2,128]{2,1,0:T(2,128)}), f32[16,2,128]{2,1,0:T(2,128)S(1)}, u32[]{:S(2)}, u32[]{:S(2)}) async-start(f32[16,2,128]{2,1,0:T(2,128)} %get-tuple-element.16), calls=%async_computation.1 | async-start | bytes 32768 | tf_op jit(solution)/shard_map/all_to_all | solution.py:231
  37.6 0.0 collective-permute-done.other_ref
  37.6 0.0 copy-done.1
  37.6 2.7 %shard_map.76 = (bf16[512,512]{1,0:T(8,128)(2,1)}, f32[4,4]{1,0:T(4,128)}, bf16[512,512]{1,0:T(8,128)(2,1)S(1)}, f32[4,4]{1,0:T(4,128)S(1)}, bf16[512,512]{1,0:T...) custom-call(s32[1]{0:T(128)} %bitcast._.core_ref, bf16[512,512]{1,0:T(8,128)(2,1)S(1)} %copy-done, ...), custom_call_target="tpu_custom_call" | custom-call | flops 11796480 | bytes 2916564 | tf_op jit(solution)/shard_map/pallas_call | solution.py:219
  40.3 0.9 %all-to-all-done.1.peaks_ref = f32[16,2,128]{2,1,0:T(2,128)S(1)} async-done(((f32[16,2,128]{2,1,0:T(2,128)}), f32[16,2,128]{2,1,0:T(2,128)S(1)}, u32[]{:S(2)}, u32[]{:S(2)}) %all-to-all-start.1) | async-done | bytes 16416 | tf_op jit(solution)/shard_map/all_to_all | solution.py:231
  41.1 1.3 %shard_map.77 = bf16[16,16,512]{2,1,0:T(8,128)(2,1)S(1)} custom-call(s32[1]{0:T(128)} %bitcast._.core_ref, bf16[32,72,128]{2,1,0:T(8,128)(2,1)S(1)} %all-to-all-done.gathered_ref, f32[2,8,512]{2,1,0:T(8,128)S(1)} %get-tuple-element.15.smooth_ref, f32[16,2,128]{2,1,0:T(2,128)S(1)} %all-to-all-done.1.peaks_ref, ...), custom_call_target="tpu_custom_call" | custom-call | flops 268435456 | bytes 1949828 | tf_op jit(solution)/shard_map/pallas_call | solution.py:219
  42.4 22.2 %all_to_all.15.parts_ref = bf16[16,16,512]{2,1,0:T(8,128)(2,1)S(1)} all-to-all(bf16[16,16,512]{2,1,0:T(8,128)(2,1)S(1)} %shard_map.77), channel_id=1, replica_groups={{256,0,288,32,320,64,352,96,384,128,416,160,448,192,480,224},{257,1,289..., dimensions={0} | all-to-all | bytes 524288 | tf_op jit(solution)/shard_map/all_to_all | solution.py:231
  64.6 0.6 shard_map.78
Async XLA Ops:
  2.6 8.6 %copy-start = (bf16[512,512]{1,0:T(8,128)(2,1)S(1)}, bf16[512,512]{1,0:T(8,128)(2,1)}, u32[]{:S(2)}) copy-start(bf16[512,512]{1,0:T(8,128)(2,1)} %query_ref.1) | copy-start | bytes 1572868
  2.6 17.5 %all-to-all-start = ((bf16[32,72,128]{2,1,0:T(8,128)(2,1)}), bf16[32,72,128]{2,1,0:T(8,128)(2,1)S(1)}, u32[]{:S(2)}, u32[]{:S(2)}) async-start(bf16[32,72,128]{2,1,0:T(8,128)(2,1)} %shard_map.74), calls=%async_computation | async-start | bytes 1179648 | tf_op jit(solution)/shard_map/all_to_all | solution.py:231
  11.2 26.4 %copy-start.1 = (bf16[512,128]{1,0:T(8,128)(2,1)S(1)}, bf16[512,128]{1,0:T(8,128)(2,1)}, u32[]{:S(2)}) copy-start(bf16[512,128]{1,0:T(8,128)(2,1)} %keyval_ref.1) | copy-start | bytes 393220
  11.2 26.3 %collective-permute-start = (bf16[512,512]{1,0:T(8,128)(2,1)S(1)}, bf16[512,512]{1,0:T(8,128)(2,1)S(1)}, u32[]{:S(2)}, u32[]{:S(2)}) collective-permute-start(bf16[512,512]{1,0:T(8,128)(2,1)S(1)} %copy-done), channel_id=1, source_target_pairs={{0,16},{16,0},{1,17},{17,1},{2,18},{18,2},{3,19},{19,3},{4,20},{20... | collective-permute-start | bytes 1572872 | tf_op jit(solution)/shard_map/ppermute | solution.py:261
  21.0 20.2 %all-to-all-start.1 = ((f32[16,2,128]{2,1,0:T(2,128)}), f32[16,2,128]{2,1,0:T(2,128)S(1)}, u32[]{:S(2)}, u32[]{:S(2)}) async-start(f32[16,2,128]{2,1,0:T(2,128)} %get-tuple-element.16), calls=%async_computation.1 | async-start | bytes 32768 | tf_op jit(solution)/shard_map/all_to_all | solution.py:231

commit v10 on v8

--- a/solution.py
+++ b/solution.py
@@ -45,11 +45,12 @@
 
 def peaks_kernel(_, tokens_hbm, query_hbm, keyval_hbm, out_hbm, *scratch):
     tokens_ref, query_ref, keyval_ref, rows_ref, both_ref, load_sems, send_sems = scratch
+    starts = range(0, query_ref.shape[0], BLOCK)
+    pairs = [(tokens_hbm, tokens_ref), (keyval_hbm, keyval_ref)]
+    pairs += [(query_hbm.at[pl.ds(b, BLOCK), :], query_ref.at[pl.ds(b, BLOCK), :]) for b in starts]
     loads = [
         pltpu.make_async_copy(source, target, load_sems.at[index])
-        for index, (source, target) in enumerate(
-            ((tokens_hbm, tokens_ref), (query_hbm, query_ref), (keyval_hbm, keyval_ref))
-        )
+        for index, (source, target) in enumerate(pairs)
     ]
     for load in loads:
         load.start()
@@ -71,9 +72,9 @@
     act = jnp.max(jnp.abs(tokens_ref[...]).astype(jnp.float32), axis=0, keepdims=True)
     acts = [act[:, base : base + BLOCK] for base in range(0, depth, BLOCK)]
     loads[1].wait()
-    loads[2].wait()
     peaks = []
-    for base in range(0, depth, BLOCK):
+    for base in starts:
+        loads[2 + base // BLOCK].wait()
         top = jnp.abs(keyval_ref[base : base + BLOCK, :])
         for left in range(0, query_ref.shape[1], BLOCK):
             top = jnp.maximum(top, jnp.abs(query_ref[base : base + BLOCK, left : left + BLOCK]))
@@ -253,7 +254,7 @@
             *(pltpu.VMEM(a.shape, a.dtype) for a in arguments),
             pltpu.VMEM((2 * columns, blocks * half, BLOCK), bf16),
             pltpu.VMEM((2 * columns, 2 * blocks, BLOCK), bf16),
-            pltpu.SemaphoreType.DMA((3,)),
+            pltpu.SemaphoreType.DMA((2 + blocks,)),
             pltpu.SemaphoreType.DMA((2,)),
         ],
     )

time: 65.7 us -> 65.9 us (level)
  no operation moved by 1% of the time
where the time goes in v10:
time: 65.9 us; the launch traced here: 65.5 us
  starting transfers between devices  28.6 us (43%)
  blocking collectives  22 us (33%)
  Pallas kernels  7.59 us (12%)
  waiting for transfers between devices  6.58 us (10%)
  between operations  0.7 us (1%)
    all_to_all x2, starting transfers between devices, exchange(): lax.all_to_all(array, axes, 0, 0, tiled=True, axis_index_groups=[order])  26.2 us
    all_to_all x1, blocking collectives, exchange(): lax.all_to_all(array, axes, 0, 0, tiled=True, axis_index_groups=[order])  22 us
    pallas_call x5, Pallas kernels, launch(): pl.pallas_call(kernel, out_shape=out_shape, in_specs=specs or [VMEM] * le...  7.59 us
    all_to_all x2, waiting for transfers between devices, exchange(): lax.all_to_all(array, axes, 0, 0, tiled=True, axis_index_groups=[order])  6.58 us
    ppermute x1, starting transfers between devices, body(): other_weight = lax.ppermute(query_weight, 'core', [(0, 1), (1, 0)])  2.46 us
  transfers between devices with their start and end apart: 3, of which 2 were waited for; matrix products, arithmetic and copies ran while one was open for 0% of the time, Pallas kernels for 5%

profile of v10, /device:TPU:1, one launch (start us, length us, event | category | flops | bytes accessed | tf_op | source)
XLA Modules:
  0.0 65.5 jit_solution(9729119236505671821)
XLA Ops:
  0.6 2.2 %shard_map.74 = bf16[32,72,128]{2,1,0:T(8,128)(2,1)} custom-call(s32[1]{0:T(128)} %bitcast._.core_ref, bf16[32,512]{1,0:T(8,128)(2,1)} %tokens_hbm.1, bf16[512,512]{1,0:T(8,128)(2,1)} %query_ref.1, bf16[512,128]{1,0:T(8,128)(2,1)} %keyval_ref.1), custom_call_target="tpu_custom_call" | custom-call | bytes 1277956 | tf_op jit(solution)/shard_map/pallas_call | solution.py:220
  2.8 0.0 copy-start
  2.8 13.1 %all-to-all-start = ((bf16[32,72,128]{2,1,0:T(8,128)(2,1)}), bf16[32,72,128]{2,1,0:T(8,128)(2,1)S(1)}, u32[]{:S(2)}, u32[]{:S(2)}) async-start(bf16[32,72,128]{2,1,0:T(8,128)(2,1)} %shard_map.74), calls=%async_computation | async-start | bytes 1179648 | tf_op jit(solution)/shard_map/all_to_all | solution.py:232
  15.9 0.0 copy-done
  15.9 0.0 copy-start.1
  15.9 2.5 %collective-permute-start = (bf16[512,512]{1,0:T(8,128)(2,1)S(1)}, bf16[512,512]{1,0:T(8,128)(2,1)S(1)}, u32[]{:S(2)}, u32[]{:S(2)}) collective-permute-start(bf16[512,512]{1,0:T(8,128)(2,1)S(1)} %copy-done), channel_id=1, source_target_pairs={{0,16},{16,0},{1,17},{17,1},{2,18},{18,2},{3,19},{19,3},{4,20},{20... | collective-permute-start | bytes 1572872 | tf_op jit(solution)/shard_map/ppermute | solution.py:262
  18.4 5.7 %all-to-all-done.gathered_ref = bf16[32,72,128]{2,1,0:T(8,128)(2,1)S(1)} async-done(((bf16[32,72,128]{2,1,0:T(8,128)(2,1)}), bf16[32,72,128]{2,1,0:T(8,128)(2,1)S(1)}, u32[]{:S(2)}, u32[]{:S(2)}) %all-to-all-start) | async-done | bytes 589856 | tf_op jit(solution)/shard_map/all_to_all | solution.py:232
  24.1 0.8 %shard_map.75 = (f32[2,8,512]{2,1,0:T(8,128)S(1)}, f32[16,2,128]{2,1,0:T(2,128)}) custom-call(bf16[32,72,128]{2,1,0:T(8,128)(2,1)S(1)} %all-to-all-done.gathered_ref), custom_call_target="tpu_custom_call" | custom-call | bytes 638976 | tf_op jit(solution)/shard_map/pallas_call | solution.py:220
  24.9 13.1 %all-to-all-start.1 = ((f32[16,2,128]{2,1,0:T(2,128)}), f32[16,2,128]{2,1,0:T(2,128)S(1)}, u32[]{:S(2)}, u32[]{:S(2)}) async-start(f32[16,2,128]{2,1,0:T(2,128)} %get-tuple-element.16), calls=%async_computation.1 | async-start | bytes 32768 | tf_op jit(solution)/shard_map/all_to_all | solution.py:232
  38.0 0.0 collective-permute-done.other_ref
  38.0 0.0 copy-done.1
  38.0 2.7 %shard_map.76 = (bf16[512,512]{1,0:T(8,128)(2,1)}, f32[4,4]{1,0:T(4,128)}, bf16[512,512]{1,0:T(8,128)(2,1)S(1)}, f32[4,4]{1,0:T(4,128)S(1)}, bf16[512,512]{1,0:T...) custom-call(s32[1]{0:T(128)} %bitcast._.core_ref, bf16[512,512]{1,0:T(8,128)(2,1)S(1)} %copy-done, ...), custom_call_target="tpu_custom_call" | custom-call | flops 11796480 | bytes 2916564 | tf_op jit(solution)/shard_map/pallas_call | solution.py:220
  40.7 0.9 %all-to-all-done.1.peaks_ref = f32[16,2,128]{2,1,0:T(2,128)S(1)} async-done(((f32[16,2,128]{2,1,0:T(2,128)}), f32[16,2,128]{2,1,0:T(2,128)S(1)}, u32[]{:S(2)}, u32[]{:S(2)}) %all-to-all-start.1) | async-done | bytes 16416 | tf_op jit(solution)/shard_map/all_to_all | solution.py:232
  41.6 1.3 %shard_map.77 = bf16[16,16,512]{2,1,0:T(8,128)(2,1)S(1)} custom-call(s32[1]{0:T(128)} %bitcast._.core_ref, bf16[32,72,128]{2,1,0:T(8,128)(2,1)S(1)} %all-to-all-done.gathered_ref, f32[2,8,512]{2,1,0:T(8,128)S(1)} %get-tuple-element.15.smooth_ref, f32[16,2,128]{2,1,0:T(2,128)S(1)} %all-to-all-done.1.peaks_ref, ...), custom_call_target="tpu_custom_call" | custom-call | flops 268435456 | bytes 1949828 | tf_op jit(solution)/shard_map/pallas_call | solution.py:220
  42.9 22.0 %all_to_all.15.parts_ref = bf16[16,16,512]{2,1,0:T(8,128)(2,1)S(1)} all-to-all(bf16[16,16,512]{2,1,0:T(8,128)(2,1)S(1)} %shard_map.77), channel_id=1, replica_groups={{288,0,320,32,352,64,384,96,416,128,448,160,480,192,256,224},{289,1,321..., dimensions={0} | all-to-all | bytes 524288 | tf_op jit(solution)/shard_map/all_to_all | solution.py:232
  64.9 0.6 shard_map.78
Async XLA Ops:
  2.8 13.1 %copy-start = (bf16[512,512]{1,0:T(8,128)(2,1)S(1)}, bf16[512,512]{1,0:T(8,128)(2,1)}, u32[]{:S(2)}) copy-start(bf16[512,512]{1,0:T(8,128)(2,1)} %query_ref.1) | copy-start | bytes 1572868
  2.8 21.2 %all-to-all-start = ((bf16[32,72,128]{2,1,0:T(8,128)(2,1)}), bf16[32,72,128]{2,1,0:T(8,128)(2,1)S(1)}, u32[]{:S(2)}, u32[]{:S(2)}) async-start(bf16[32,72,128]{2,1,0:T(8,128)(2,1)} %shard_map.74), calls=%async_computation | async-start | bytes 1179648 | tf_op jit(solution)/shard_map/all_to_all | solution.py:232
  15.9 22.1 %copy-start.1 = (bf16[512,128]{1,0:T(8,128)(2,1)S(1)}, bf16[512,128]{1,0:T(8,128)(2,1)}, u32[]{:S(2)}) copy-start(bf16[512,128]{1,0:T(8,128)(2,1)} %keyval_ref.1) | copy-start | bytes 393220
  15.9 22.1 %collective-permute-start = (bf16[512,512]{1,0:T(8,128)(2,1)S(1)}, bf16[512,512]{1,0:T(8,128)(2,1)S(1)}, u32[]{:S(2)}, u32[]{:S(2)}) collective-permute-start(bf16[512,512]{1,0:T(8,128)(2,1)S(1)} %copy-done), channel_id=1, source_target_pairs={{0,16},{16,0},{1,17},{17,1},{2,18},{18,2},{3,19},{19,3},{4,20},{20... | collective-permute-start | bytes 1572872 | tf_op jit(solution)/shard_map/ppermute | solution.py:262
  24.9 16.7 %all-to-all-start.1 = ((f32[16,2,128]{2,1,0:T(2,128)}), f32[16,2,128]{2,1,0:T(2,128)S(1)}, u32[]{:S(2)}, u32[]{:S(2)}) async-start(f32[16,2,128]{2,1,0:T(2,128)} %get-tuple-element.16), calls=%async_computation.1 | async-start | bytes 32768 | tf_op jit(solution)/shard_map/all_to_all | solution.py:232
